TPU v7x, 128 devices: a whole 4x4x4 slice. The times are simulated.
128 devices in a mesh: rep: 4 (over x), ep: 32 (over y, z, core).
Axes of the slice: x: 4, y: 4, z: 4, core: 2. Of those that a mesh axis runs over, the one named last changes fastest.
Arguments:
- q_latent: bfloat16 [1024, 128, 512], P(('rep', 'ep')), may hold values from -6 to 6
- q_rope: bfloat16 [1024, 128, 64], P(('rep', 'ep')), may hold values from -104 to 104
- cache_latent: bfloat16 [1024, 128, 512], P(('rep', 'ep')), may hold values from -6 to 6
- cache_rope: bfloat16 [1024, 128, 64], P(('rep', 'ep')), may hold values from -6 to 6
- cache_len: int32 [1024], P(('rep', 'ep')), may hold values from 32 to 128, as said below
- stream: bfloat16 [1024, 7168], P(('rep', 'ep')), may hold values from -6 to 6
- norm_gain: float32 [7168], replicated, may hold values from 0.1 to 1.9
- expert_ids: int32 [1024, 8], P(('rep', 'ep')), may hold values from 0 to 63, all different within a row; in each aligned block of 8 rows (0 to 7, 8 to 15, ...) at most 2 rows name the same one
- route_weights: bfloat16 [1024, 8], P(('rep', 'ep')), may hold values from 0.099609375 to 1
- w_gate: bfloat16 [64, 7168, 1024], P('ep', None, 'rep'), may hold values from -0.0625 to 0.0625
- w_up: bfloat16 [64, 7168, 1024], P('ep', None, 'rep'), may hold values from -0.0625 to 0.0625
- w_down: bfloat16 [64, 1024, 7168], P('ep', 'rep'), may hold values from -0.1875 to 0.1875
Outputs:
- attn_latent: bfloat16 [1024, 128, 512], P(('rep', 'ep'))
- layer_out: bfloat16 [1024, 7168], P(('rep', 'ep'))
Inputs may be any that keep to these rules, and one draw needn't show every extreme that they name: `expert_ids`: each row names 8 different experts; within the rows of one device no expert is named by more than 2 rows, a bound that some block reaches. `cache_len`: some row has all 128 positions live.
All inputs are finite; a program needn't handle non-finite values.
Results may differ from a plain program's by a relative error of at most 0.01.
Values may be sent and summed in bfloat16 or wider, within the bound.
No kernel may reach another device: no remote copies, remote signals or barrier semaphores. Data moves between devices by JAX's collectives and lax.ppermute only.
A program may use at most 128 MiB of HBM per device.

v0:
```python
import jax
import jax.numpy as jnp
from jax import lax
from jax.experimental import pallas as pl
from jax.experimental.pallas import tpu as pltpu
from jax.sharding import Mesh
from jax.sharding import PartitionSpec as P


TORUS = ("rep", "ep_0", "ep_1", "ep_2")
EP = ("ep_0", "ep_1", "ep_2")


score_scale = 192.0 ** (-0.5)
norm_eps = 1e-06
meta_lanes = 128
vmem_share = 16 << 20

PHASE_AXES = ((2, 1, 0), (0, 2, 1))


def torus_pairs(phase, step):
    sizes = [lax.axis_size(a) for a in TORUS]
    pairs = []
    for src in range(sizes[0] * sizes[1] * sizes[2] * sizes[3]):
        rest, core = divmod(src, sizes[3])
        rest, z = divmod(rest, sizes[2])
        x, y = divmod(rest, sizes[1])
        at = [x, y, z]
        axis = PHASE_AXES[core][phase]
        at[axis] = (at[axis] + step) % sizes[axis]
        pairs.append((src, ((at[0] * sizes[1] + at[1]) * sizes[2] + at[2]) * sizes[3] + core))
    return pairs


def move(block, phase, step):
    return lax.ppermute(block, TORUS, torus_pairs(phase, step))


def swap(block):
    return lax.ppermute(block, "ep_2", [(0, 1), (1, 0)])


def after(values):
    return lax.optimization_barrier(values)


def widen(block):
    return block.astype(jnp.float32)


def narrow(block):
    return block.astype(jnp.bfloat16)


def spread_direct(block, phase):
    return [block, move(block, phase, 1), move(block, phase, -1), move(block, phase, 2)]


def fold_direct(own, behind, ahead, across, phase):
    got = [move(behind, phase, -1), move(ahead, phase, 1), move(across, phase, 2)]
    return widen(own) + widen(got[0]) + widen(got[1]) + widen(got[2])


def spread_ring(block, phase):
    half = block.shape[0] // 2
    behind = move(block, phase, 1)
    ahead = move(block, phase, -1)
    across_a = move(behind[:half], phase, 1)
    across_b = move(ahead[half:], phase, -1)
    return [block, behind, ahead, across_a, across_b]


def fold_ring(own, behind, ahead, across_a, across_b, phase):
    half = own.shape[0] // 2
    via_a = move(narrow(across_a), phase, -1)
    via_b = move(narrow(across_b), phase, 1)
    behind = jnp.concatenate([narrow(widen(behind[:half]) + widen(via_a)), narrow(behind[half:])])
    ahead = jnp.concatenate([narrow(ahead[:half]), narrow(widen(ahead[half:]) + widen(via_b))])
    got_a = move(behind, phase, -1)
    got_b = move(ahead, phase, 1)
    return widen(own) + widen(got_a) + widen(got_b)


def prepare(stream, norm_gain, expert_ids, route_weights):
    row_count, width = stream.shape

    def kernel(stream_ref, gain_ref, ids_ref, weights_ref, out_ref):
        rows = widen(stream_ref[...])
        scale = lax.rsqrt(jnp.mean(rows * rows, axis=-1, keepdims=True) + norm_eps)
        out_ref[:, :width] = narrow(rows * scale * gain_ref[...])
        ids = ids_ref[...]
        weights = widen(weights_ref[...])
        lane = lax.broadcasted_iota(jnp.int32, (row_count, meta_lanes), 1)
        table = jnp.zeros((row_count, meta_lanes), jnp.float32)
        for k in range(ids.shape[1]):
            table = jnp.where(lane == ids[:, k : k + 1], weights[:, k : k + 1], table)
        out_ref[:, width:] = narrow(table)

    return pl.pallas_call(
        kernel,
        out_shape=jax.ShapeDtypeStruct((row_count, width + meta_lanes), jnp.bfloat16),
        name="prepare",
    )(stream, norm_gain.reshape(1, -1), expert_ids, route_weights)


def resident(*arrays):
    count = len(arrays)

    def kernel(*refs):
        sources, targets, sems = refs[:count], refs[count : 2 * count], refs[2 * count]
        copies = [
            pltpu.make_async_copy(sources[i], targets[i], sems.at[i]) for i in range(count)
        ]
        for copy in copies:
            copy.start()
        for copy in copies:
            copy.wait()

    return pl.pallas_call(
        kernel,
        in_specs=[pl.BlockSpec(memory_space=pltpu.HBM)] * count,
        out_specs=[pl.BlockSpec(memory_space=pltpu.VMEM)] * count,
        out_shape=[pltpu.VMEM(a.shape, a.dtype) for a in arrays],
        scratch_shapes=[pltpu.SemaphoreType.DMA((count,))],
        compiler_params=pltpu.CompilerParams(vmem_limit_bytes=vmem_share),
        name="resident",
    )(*[pltpu.with_memory_space_constraint(a, pltpu.HBM) for a in arrays])


def hidden_of(blocks, w_gate, w_up, first_expert):
    local_count, width, units = w_gate.shape
    steps = 2
    tile = width // steps
    sizes = [b.shape[0] for b in blocks]
    total = sum(sizes)
    count = len(blocks)

    def kernel(first_ref, *refs):
        rows_refs, meta_refs = refs[:count], refs[count : 2 * count]
        gate_ref, up_ref, out_ref, acc_ref = refs[2 * count :]
        step = pl.program_id(0)

        @pl.when(step == 0)
        def _():
            acc_ref[...] = jnp.zeros_like(acc_ref)

        rows = jnp.concatenate([r[...] for r in rows_refs], axis=0)
        for e in range(local_count):
            gate = gate_ref[e, pl.ds(step * tile, tile), :]
            up = up_ref[e, pl.ds(step * tile, tile), :]
            acc_ref[2 * e] += jnp.dot(rows, gate, preferred_element_type=jnp.float32)
            acc_ref[2 * e + 1] += jnp.dot(rows, up, preferred_element_type=jnp.float32)

        @pl.when(step == steps - 1)
        def _():
            meta = widen(jnp.concatenate([r[...] for r in meta_refs], axis=0))
            lane = lax.broadcasted_iota(jnp.int32, meta.shape, 1)
            for e in range(local_count):
                mine = jnp.where(lane == first_ref[0] + e, meta, 0.0)
                share = jnp.sum(mine, axis=1, keepdims=True)
                act = jax.nn.silu(acc_ref[2 * e]) * acc_ref[2 * e + 1] * share
                out_ref[:, e * units : (e + 1) * units] = narrow(act)

    return pl.pallas_call(
        kernel,
        grid=(steps,),
        in_specs=[pl.BlockSpec(memory_space=pltpu.SMEM)]
        + [pl.BlockSpec((n, tile), lambda k: (0, k)) for n in sizes]
        + [pl.BlockSpec((n, meta_lanes), lambda k: (0, width // meta_lanes)) for n in sizes]
        + [pl.BlockSpec(memory_space=pltpu.VMEM)] * 2,
        out_specs=pl.BlockSpec((total, local_count * units), lambda k: (0, 0)),
        out_shape=jax.ShapeDtypeStruct((total, local_count * units), jnp.bfloat16),
        scratch_shapes=[pltpu.VMEM((2 * local_count, total, units), jnp.float32)],
        compiler_params=pltpu.CompilerParams(vmem_limit_bytes=vmem_share),
        cost_estimate=pl.CostEstimate(
            flops=4 * total * width * units * local_count,
            transcendentals=total * units * local_count,
            bytes_accessed=4 * width * units * local_count + 2 * total * width,
        ),
        name="hidden",
    )(first_expert, *blocks, *blocks, w_gate, w_up)


def outputs_of(hidden, block, sizes, down, got=None):
    width = down.shape[2]
    inner = hidden.shape[1]
    steps = 4
    tile = width // steps
    total = sum(sizes)

    def kernel(*refs):
        hidden_ref, down_ref = refs[:2]
        out_refs = refs[-len(sizes) :]
        here = pl.ds(pl.multiple_of(pl.program_id(0) * tile, 128), tile)
        hidden_rows = hidden_ref[...]
        units = inner // down_ref.shape[0]
        part = jnp.zeros((total, tile), jnp.float32)
        for e in range(down_ref.shape[0]):
            part = part + jnp.dot(
                hidden_rows[:, e * units : (e + 1) * units],
                down_ref[e, :, here],
                preferred_element_type=jnp.float32,
            )
        if got is not None:
            part = part + widen(refs[2][...])
        at = 0
        for n, out_ref in zip(sizes, out_refs):
            out_ref[...] = narrow(part[at : at + n])
            at += n

    specs = [
        pl.BlockSpec((total, inner), lambda n: (block, 0)),
        pl.BlockSpec(memory_space=pltpu.VMEM),
    ]
    operands = [hidden, down]
    if got is not None:
        specs.append(pl.BlockSpec((total, tile), lambda n: (0, n)))
        operands.append(got)
    return pl.pallas_call(
        kernel,
        grid=(steps,),
        in_specs=specs,
        out_specs=[pl.BlockSpec((n, tile), lambda n: (0, n)) for n in sizes],
        out_shape=[jax.ShapeDtypeStruct((n, width), jnp.bfloat16) for n in sizes],
        compiler_params=pltpu.CompilerParams(vmem_limit_bytes=vmem_share),
        cost_estimate=pl.CostEstimate(
            flops=2 * total * inner * width,
            transcendentals=0,
            bytes_accessed=2 * inner * width + 4 * total * width,
        ),
        name="outputs",
    )(*operands)


def attention(q_latent, q_rope, cache_latent, cache_rope, cache_len):
    scores = (
        jnp.einsum("ihl,itl->iht", q_latent, cache_latent, preferred_element_type=jnp.float32)
        + jnp.einsum("ihr,itr->iht", q_rope, cache_rope, preferred_element_type=jnp.float32)
    ) * score_scale
    valid_mask = (
        jnp.arange(cache_latent.shape[1], dtype=jnp.int32)[None, None, :] < cache_len[:, None, None]
    )
    scores = jnp.where(valid_mask, scores, -1e30)
    top_score = jnp.max(scores, axis=-1, keepdims=True)
    exponent = jnp.where(valid_mask, jnp.exp(scores - top_score), 0.0)
    attn_weights = (exponent / jnp.sum(exponent, axis=-1, keepdims=True)).astype(jnp.bfloat16)
    return jnp.einsum(
        "iht,itl->ihl", attn_weights, cache_latent, preferred_element_type=jnp.float32
    ).astype(jnp.bfloat16)


def layer(
    q_latent,
    q_rope,
    cache_latent,
    cache_rope,
    cache_len,
    stream,
    norm_gain,
    expert_ids,
    route_weights,
    w_gate,
    w_up,
    w_down,
):
    row_count, _ = stream.shape
    local_count = w_gate.shape[0]
    first_expert = (lax.axis_index(EP) * local_count).astype(jnp.int32).reshape(1)
    stream_f = widen(stream)
    payload = prepare(stream, norm_gain, expert_ids, route_weights)

    line = jnp.concatenate(spread_direct(payload, 0))
    plane = jnp.concatenate(spread_ring(line, 1))
    block = plane.shape[0]
    half = block // 2
    behind = move(plane, 2, 1)
    ahead = move(plane, 2, -1)
    plane_2 = swap(plane)
    w_gate, w_up, down = resident(w_gate, w_up, w_down)
    hid_own = hidden_of([plane, plane_2], w_gate, w_up, first_expert)
    (own_2,) = outputs_of(hid_own, 1, [block], down)
    own_got = swap(own_2)
    (mine,) = outputs_of(hid_own, 0, [block], down, own_got)

    behind, ahead, mine = after((behind, ahead, mine))
    across_a = move(behind[:half], 2, 1)
    across_b = move(ahead[half:], 2, -1)
    behind_2 = swap(behind)
    ahead_2 = swap(ahead)
    hid_near = hidden_of([behind, ahead], w_gate, w_up, first_expert)
    behind_2, ahead_2, hid_near = after((behind_2, ahead_2, hid_near))
    hid_near_2 = hidden_of([behind_2, ahead_2], w_gate, w_up, first_expert)

    across_a, across_b, hid_near_2 = after((across_a, across_b, hid_near_2))
    across_a2 = swap(across_a)
    across_b2 = swap(across_b)
    (near_2,) = outputs_of(hid_near_2, 0, [2 * block], down)
    across_a2, across_b2, near_2 = after((across_a2, across_b2, near_2))
    near_got = swap(near_2)
    hid_far = hidden_of([across_a, across_b, across_a2, across_b2], w_gate, w_up, first_expert)
    (far_2,) = outputs_of(hid_far, 1, [block], down)
    hid_near, far_2 = after((hid_near, far_2))
    far_got = swap(far_2)
    near_a, near_b = outputs_of(hid_near, 0, [block, block], down, near_got)
    hid_far, near_a, near_b = after((hid_far, near_a, near_b))
    far_a, far_b = outputs_of(hid_far, 0, [half, half], down, far_got)

    plane_sum = fold_ring(mine, near_a, near_b, far_a, far_b, 2)
    quarter = block // 4
    plane_sum = narrow(plane_sum)
    line_sum = fold_ring(
        plane_sum[:quarter],
        plane_sum[quarter : 2 * quarter],
        plane_sum[2 * quarter : 3 * quarter],
        plane_sum[3 * quarter : 3 * quarter + quarter // 2],
        plane_sum[3 * quarter + quarter // 2 :],
        1,
    )
    line_sum = narrow(line_sum)
    expert_sum = fold_direct(
        line_sum[:row_count],
        line_sum[row_count : 2 * row_count],
        line_sum[2 * row_count : 3 * row_count],
        line_sum[3 * row_count :],
        0,
    )
    layer_out = narrow(stream_f + expert_sum)
    attn_latent = attention(q_latent, q_rope, cache_latent, cache_rope, cache_len)
    return (attn_latent, layer_out)


def solution(mesh):
    sizes = mesh.shape
    torus = Mesh(mesh.devices.reshape(sizes["rep"], 4, 4, 2), TORUS)
    return jax.shard_map(
        layer,
        mesh=torus,
        in_specs=(
            P(TORUS, None, None),
            P(TORUS, None, None),
            P(TORUS, None, None),
            P(TORUS, None, None),
            P(TORUS),
            P(TORUS, None),
            P(),
            P(TORUS, None),
            P(TORUS, None),
            P(EP, None, "rep"),
            P(EP, None, "rep"),
            P(EP, "rep", None),
        ),
        out_specs=(P(TORUS, None, None), P(TORUS, None)),
        check_vma=False,
    )
```

profile of v0, /device:TPU:30, one launch (start us, length us, event | category | flops | bytes accessed | tf_op | source)
XLA Modules:
  0.0 178.8 jit_solution(7857431233471706648)
XLA Ops:
  0.6 1.8 %prepare.1 = bf16[8,7296]{1,0:T(8,128)(2,1)} custom-call(bf16[8,7168]{1,0:T(8,128)(2,1)} %stream_ref.1, f32[1,7168]{1,0:T(1,128)} %bitcast.9, s32[8,8]{1,0:T(8,128)} %ids_ref.1, bf16[8,8]{1,0:T(8,128)(2,1)} %weights_ref.1), custom_call_target="tpu_custom_call" | custom-call | tf_op jit(solution)/shard_map/prepare/pallas_call | solution.py:100
  2.5 3.9 %collective-permute-start.2 = (bf16[8,7296]{1,0:T(8,128)(2,1)}, bf16[8,7296]{1,0:T(8,128)(2,1)S(1)}, u32[]{:S(2)}, u32[]{:S(2)}) collective-permute-start(bf16[8,7296]{1,0:T(8,128)(2,1)} %prepare.1), channel_id=1, source_target_pairs={{0,4},{1,65},{2,6},{3,67},{4,0},{5,69},{6,2},{7,71},{8,12},{9,73},... | collective-permute-start | bytes 350216 | tf_op jit(solution)/shard_map/ppermute | solution.py:37
  9.4 2.3 %collective-permute-done.1 = bf16[8,7296]{1,0:T(8,128)(2,1)S(1)} collective-permute-done((bf16[8,7296]{1,0:T(8,128)(2,1)}, bf16[8,7296]{1,0:T(8,128)(2,1)S(1)}, u32[]{:S(2)}, u32[]{:S(2)}) %collective-permute-start.1) | collective-permute-done | bytes 116768 | tf_op jit(solution)/shard_map/ppermute | solution.py:37
  15.1 2.5 %collective-permute-start.3 = (bf16[32,7296]{1,0:T(8,128)(2,1)S(1)}, bf16[32,7296]{1,0:T(8,128)(2,1)S(1)}, u32[]{:S(2)}, u32[]{:S(2)}) collective-permute-start(bf16[32,7296]{1,0:T(8,128)(2,1)S(1)} %pad_maximum_fusion.2), channel_id=1, source_target_pairs={{0,8},{1,3},{2,10},{3,5},{4,12},{5,7},{6,14},{7,1},{8,16},{9,11},{... | collective-permute-start | bytes 1400840 | tf_op jit(solution)/shard_map/ppermute | solution.py:37
  17.6 6.5 %collective-permute-done.4 = bf16[32,7296]{1,0:T(8,128)(2,1)S(1)} collective-permute-done((bf16[32,7296]{1,0:T(8,128)(2,1)S(1)}, bf16[32,7296]{1,0:T(8,128)(2,1)S(1)}, u32[]{:S(2)}, u32[]{:S(2)}) %collective-permute-start.4) | collective-permute-done | bytes 466976 | tf_op jit(solution)/shard_map/ppermute | solution.py:37
  24.2 3.3 %collective-permute-start.5 = (bf16[16,7296]{1,0:T(8,128)(2,1)S(1)}, bf16[16,7296]{1,0:T(8,128)(2,1)S(1)}, u32[]{:S(2)}, u32[]{:S(2)}) collective-permute-start(bf16[16,7296]{1,0:T(8,128)(2,1)S(1)} %slice.82), channel_id=1, source_target_pairs={{0,8},{1,3},{2,10},{3,5},{4,12},{5,7},{6,14},{7,1},{8,16},{9,11},{... | collective-permute-start | bytes 700424 | tf_op jit(solution)/shard_map/ppermute | solution.py:37
  27.6 3.5 %collective-permute-done.5 = bf16[16,7296]{1,0:T(8,128)(2,1)S(1)} collective-permute-done((bf16[16,7296]{1,0:T(8,128)(2,1)S(1)}, bf16[16,7296]{1,0:T(8,128)(2,1)S(1)}, u32[]{:S(2)}, u32[]{:S(2)}) %collective-permute-start.5) | collective-permute-done | bytes 233504 | tf_op jit(solution)/shard_map/ppermute | solution.py:37
  31.6 7.3 %resident.1 = (bf16[2,7168,256]{2,1,0:T(8,128)(2,1)S(1)}, bf16[2,7168,256]{2,1,0:T(8,128)(2,1)S(1)}, bf16[2,256,7168]{2,1,0:T(8,128)(2,1)S(1)}) custom-call(bf16[2,7168,256]{2,1,0:T(8,128)(2,1)} %refs_0_.1, bf16[2,7168,256]{2,1,0:T(8,128)(2,1)} %refs_1_.1, bf16[2,256,7168]{2,1,0:T(8,128)(2,1)} %refs_2_.1), custom_call_target="tpu_custom_call" | custom-call | tf_op jit(solution)/shard_map/resident/pallas_call | solution.py:120
  38.9 5.7 %hidden.4.refs_0_ = bf16[256,512]{1,0:T(8,128)(2,1)S(1)} custom-call(s32[1]{0:T(128)} %bitcast.1.first_ref, bf16[128,7296]{1,0:T(8,128)(2,1)S(1)} %constant_dynamic-update-slice_fusion.refs_0_.refs_2_, bf16[128,7296]{1,0:T(8,128)(2,1)} %collective-permute-done.9.refs_1_.refs_3_, bf16[128,7296]{1,0:T(8,128)(2,1)S(1)} %constant_dynamic-update-slice_fusion.refs_0_.refs_2_, ...), custom_call_target="tpu_custom_call" | custom-call | flops 3758096384 | bytes 18350080 | tf_op jit(solution)/shard_map/hidden/pallas_call | solution.py:165
  44.6 1.8 %outputs.6 = bf16[128,7168]{1,0:T(8,128)(2,1)S(1)} custom-call(bf16[256,512]{1,0:T(8,128)(2,1)S(1)} %hidden.4.refs_0_, bf16[2,256,7168]{2,1,0:T(8,128)(2,1)S(1)} %get-tuple-element.28.refs_1_), custom_call_target="tpu_custom_call" | custom-call | flops 939524096 | bytes 11010048 | tf_op jit(solution)/shard_map/outputs/pallas_call | solution.py:220
  47.8 2.4 %collective-permute-start.7 = (bf16[128,7296]{1,0:T(8,128)(2,1)S(1)}, bf16[128,7296]{1,0:T(8,128)(2,1)S(1)}, u32[]{:S(2)}, u32[]{:S(2)}) collective-permute-start(bf16[128,7296]{1,0:T(8,128)(2,1)S(1)} %constant_dynamic-update-slice_fusion.refs_0_.refs_2_), channel_id=1, source_target_pairs={{0,32},{1,9},{2,34},{3,11},{4,36},{5,13},{6,38},{7,15},{8,40},{9,1... | collective-permute-start | bytes 5603336 | tf_op jit(solution)/shard_map/ppermute | solution.py:37
  50.4 2.0 %outputs.7 = bf16[128,7168]{1,0:T(8,128)(2,1)S(1)} custom-call(bf16[256,512]{1,0:T(8,128)(2,1)S(1)} %hidden.4.refs_0_, bf16[2,256,7168]{2,1,0:T(8,128)(2,1)S(1)} %get-tuple-element.28.refs_1_, bf16[128,7168]{1,0:T(8,128)(2,1)S(1)} %collective-permute-done.10.refs_2_), custom_call_target="tpu_custom_call" | custom-call | flops 939524096 | bytes 11010048 | tf_op jit(solution)/shard_map/outputs/pallas_call | solution.py:220
  52.4 19.4 %collective-permute-done.8.refs_1_.refs_3_ = bf16[128,7296]{1,0:T(8,128)(2,1)S(1)} collective-permute-done((bf16[128,7296]{1,0:T(8,128)(2,1)S(1)}, bf16[128,7296]{1,0:T(8,128)(2,1)S(1)}, u32[]{:S(2)}, u32[]{:S(2)}) %collective-permute-start.8) | collective-permute-done | bytes 1867808 | tf_op jit(solution)/shard_map/ppermute | solution.py:37
  72.6 3.3 %collective-permute-start.11 = (bf16[64,7296]{1,0:T(8,128)(2,1)S(1)}, bf16[64,7296]{1,0:T(8,128)(2,1)S(1)}, u32[]{:S(2)}, u32[]{:S(2)}) collective-permute-start(bf16[64,7296]{1,0:T(8,128)(2,1)S(1)} %slice.65), channel_id=1, source_target_pairs={{0,32},{1,9},{2,34},{3,11},{4,36},{5,13},{6,38},{7,15},{8,40},{9,1... | collective-permute-start | bytes 2801672 | tf_op jit(solution)/shard_map/ppermute | solution.py:37
  76.0 4.8 %hidden.5.refs_0_ = bf16[256,512]{1,0:T(8,128)(2,1)S(1)} custom-call(s32[1]{0:T(128)} %bitcast.1.first_ref, bf16[128,7296]{1,0:T(8,128)(2,1)S(1)} %collective-permute-done.7.refs_0_.refs_2_, bf16[128,7296]{1,0:T(8,128)(2,1)S(1)} %collective-permute-done.8.refs_1_.refs_3_, bf16[128,7296]{1,0:T(8,128)(2,1)S(1)} %collective-permute-done.7.refs_0_.refs_2_, ...), custom_call_target="tpu_custom_call" | custom-call | flops 3758096384 | bytes 18350080 | tf_op jit(solution)/shard_map/hidden/pallas_call | solution.py:165
  80.7 4.8 %hidden.6.refs_0_ = bf16[256,512]{1,0:T(8,128)(2,1)S(1)} custom-call(s32[1]{0:T(128)} %bitcast.1.first_ref, bf16[128,7296]{1,0:T(8,128)(2,1)S(1)} %collective-permute-done.13.refs_0_.refs_2_, bf16[128,7296]{1,0:T(8,128)(2,1)S(1)} %collective-permute-done.14.refs_1_.refs_3_, bf16[128,7296]{1,0:T(8,128)(2,1)S(1)} %collective-permute-done.13.refs_0_.refs_2_, ...), custom_call_target="tpu_custom_call" | custom-call | flops 3758096384 | bytes 18350080 | tf_op jit(solution)/shard_map/hidden/pallas_call | solution.py:165
  87.8 2.9 %outputs.8 = bf16[256,7168]{1,0:T(8,128)(2,1)S(1)} custom-call(bf16[256,512]{1,0:T(8,128)(2,1)S(1)} %hidden.6.refs_0_, bf16[2,256,7168]{2,1,0:T(8,128)(2,1)S(1)} %get-tuple-element.28.refs_1_), custom_call_target="tpu_custom_call" | custom-call | flops 1879048192 | bytes 14680064 | tf_op jit(solution)/shard_map/outputs/pallas_call | solution.py:220
  91.2 5.0 %hidden.7.refs_0_ = bf16[256,512]{1,0:T(8,128)(2,1)S(1)} custom-call(s32[1]{0:T(128)} %bitcast.1.first_ref, bf16[64,7296]{1,0:T(8,128)(2,1)S(1)} %collective-permute-done.11.refs_0_.refs_4_, bf16[64,7296]{1,0:T(8,128)(2,1)S(1)} %collective-permute-done.12.refs_1_.refs_5_, bf16[64,7296]{1,0:T(8,128)(2,1)S(1)} %collective-permute-done.15.refs_2_.refs_6_, ...), custom_call_target="tpu_custom_call" | custom-call | flops 3758096384 | bytes 18350080 | tf_op jit(solution)/shard_map/hidden/pallas_call | solution.py:165
  96.2 1.8 %outputs.9 = bf16[128,7168]{1,0:T(8,128)(2,1)S(1)} custom-call(bf16[256,512]{1,0:T(8,128)(2,1)S(1)} %hidden.7.refs_0_, bf16[2,256,7168]{2,1,0:T(8,128)(2,1)S(1)} %get-tuple-element.28.refs_1_), custom_call_target="tpu_custom_call" | custom-call | flops 939524096 | bytes 11010048 | tf_op jit(solution)/shard_map/outputs/pallas_call | solution.py:220
  98.5 3.2 %outputs.10 = (bf16[128,7168]{1,0:T(8,128)(2,1)S(1)}, bf16[128,7168]{1,0:T(8,128)(2,1)S(1)}) custom-call(bf16[256,512]{1,0:T(8,128)(2,1)S(1)} %hidden.5.refs_0_, bf16[2,256,7168]{2,1,0:T(8,128)(2,1)S(1)} %get-tuple-element.28.refs_1_, bf16[256,7168]{1,0:T(8,128)(2,1)S(1)} %collective-permute-done.17.refs_2_), custom_call_target="tpu_custom_call" | custom-call | flops 1879048192 | bytes 14680064 | tf_op jit(solution)/shard_map/outputs/pallas_call | solution.py:220
  101.9 2.0 %outputs.11 = (bf16[64,7168]{1,0:T(8,128)(2,1)S(1)}, bf16[64,7168]{1,0:T(8,128)(2,1)S(1)}) custom-call(bf16[256,512]{1,0:T(8,128)(2,1)S(1)} %hidden.7.refs_0_, bf16[2,256,7168]{2,1,0:T(8,128)(2,1)S(1)} %get-tuple-element.28.refs_1_, bf16[128,7168]{1,0:T(8,128)(2,1)S(1)} %collective-permute-done.18.refs_2_), custom_call_target="tpu_custom_call" | custom-call | flops 939524096 | bytes 11010048 | tf_op jit(solution)/shard_map/outputs/pallas_call | solution.py:220
  103.9 3.6 %collective-permute-start.21 = (bf16[64,7168]{1,0:T(8,128)(2,1)S(1)}, bf16[64,7168]{1,0:T(8,128)(2,1)S(1)}, u32[]{:S(2)}, u32[]{:S(2)}) collective-permute-start(bf16[64,7168]{1,0:T(8,128)(2,1)S(1)} %get-tuple-element.49), channel_id=1, source_target_pairs={{0,32},{1,9},{2,34},{3,11},{4,36},{5,13},{6,38},{7,15},{8,40},{9,1... | collective-permute-start | bytes 2752520 | tf_op jit(solution)/shard_map/ppermute | solution.py:37
  107.7 10.7 %collective-permute-done.21 = bf16[64,7168]{1,0:T(8,128)(2,1)S(1)} collective-permute-done((bf16[64,7168]{1,0:T(8,128)(2,1)S(1)}, bf16[64,7168]{1,0:T(8,128)(2,1)S(1)}, u32[]{:S(2)}, u32[]{:S(2)}) %collective-permute-start.21) | collective-permute-done | bytes 917536 | tf_op jit(solution)/shard_map/ppermute | solution.py:37
  118.7 3.8 %collective-permute-start.22 = (bf16[128,7168]{1,0:T(8,128)(2,1)S(1)}, bf16[128,7168]{1,0:T(8,128)(2,1)S(1)}, u32[]{:S(2)}, u32[]{:S(2)}) collective-permute-start(bf16[128,7168]{1,0:T(8,128)(2,1)S(1)} %pad_maximum_fusion.1), channel_id=1, source_target_pairs={{0,32},{1,9},{2,34},{3,11},{4,36},{5,13},{6,38},{7,15},{8,40},{9,1... | collective-permute-start | bytes 5505032 | tf_op jit(solution)/shard_map/ppermute | solution.py:37
  123.2 20.1 %collective-permute-done.22 = bf16[128,7168]{1,0:T(8,128)(2,1)S(1)} collective-permute-done((bf16[128,7168]{1,0:T(8,128)(2,1)S(1)}, bf16[128,7168]{1,0:T(8,128)(2,1)S(1)}, u32[]{:S(2)}, u32[]{:S(2)}) %collective-permute-start.22) | collective-permute-done | bytes 1835040 | tf_op jit(solution)/shard_map/ppermute | solution.py:37
  143.2 4.3 %collective-permute-done.20 = bf16[128,7168]{1,0:T(8,128)(2,1)S(1)} collective-permute-done((bf16[128,7168]{1,0:T(8,128)(2,1)S(1)}, bf16[128,7168]{1,0:T(8,128)(2,1)S(1)}, u32[]{:S(2)}, u32[]{:S(2)}) %collective-permute-start.20) | collective-permute-done | bytes 1835040 | tf_op jit(solution)/shard_map/ppermute | solution.py:37
  148.6 3.4 %collective-permute-start.25 = (bf16[16,7168]{1,0:T(8,128)(2,1)S(1)}, bf16[16,7168]{1,0:T(8,128)(2,1)S(1)}, u32[]{:S(2)}, u32[]{:S(2)}) collective-permute-start(bf16[16,7168]{1,0:T(8,128)(2,1)S(1)} %get-tuple-element.53), channel_id=1, source_target_pairs={{0,8},{1,3},{2,10},{3,5},{4,12},{5,7},{6,14},{7,1},{8,16},{9,11},{... | collective-permute-start | bytes 688136 | tf_op jit(solution)/shard_map/ppermute | solution.py:37
  152.5 3.4 %collective-permute-done.23 = bf16[16,7168]{1,0:T(8,128)(2,1)S(1)} collective-permute-done((bf16[16,7168]{1,0:T(8,128)(2,1)S(1)}, bf16[16,7168]{1,0:T(8,128)(2,1)S(1)}, u32[]{:S(2)}, u32[]{:S(2)}) %collective-permute-start.23) | collective-permute-done | bytes 229408 | tf_op jit(solution)/shard_map/ppermute | solution.py:37
  156.1 3.4 %collective-permute-start.26 = (bf16[32,7168]{1,0:T(8,128)(2,1)S(1)}, bf16[32,7168]{1,0:T(8,128)(2,1)S(1)}, u32[]{:S(2)}, u32[]{:S(2)}) collective-permute-start(bf16[32,7168]{1,0:T(8,128)(2,1)S(1)} %pad_maximum_fusion.4), channel_id=1, source_target_pairs={{0,8},{1,3},{2,10},{3,5},{4,12},{5,7},{6,14},{7,1},{8,16},{9,11},{... | collective-permute-start | bytes 1376264 | tf_op jit(solution)/shard_map/ppermute | solution.py:37
  160.2 5.2 %collective-permute-done.26 = bf16[32,7168]{1,0:T(8,128)(2,1)S(1)} collective-permute-done((bf16[32,7168]{1,0:T(8,128)(2,1)S(1)}, bf16[32,7168]{1,0:T(8,128)(2,1)S(1)}, u32[]{:S(2)}, u32[]{:S(2)}) %collective-permute-start.26) | collective-permute-done | bytes 458784 | tf_op jit(solution)/shard_map/ppermute | solution.py:37
  165.5 3.8 %collective-permute-done.24 = bf16[32,7168]{1,0:T(8,128)(2,1)S(1)} collective-permute-done((bf16[32,7168]{1,0:T(8,128)(2,1)S(1)}, bf16[32,7168]{1,0:T(8,128)(2,1)S(1)}, u32[]{:S(2)}, u32[]{:S(2)}) %collective-permute-start.24) | collective-permute-done | bytes 458784 | tf_op jit(solution)/shard_map/ppermute | solution.py:37
  174.4 2.5 %collective-permute-done.29 = bf16[8,7168]{1,0:T(8,128)(2,1)S(1)} collective-permute-done((bf16[8,7168]{1,0:T(8,128)(2,1)S(1)}, bf16[8,7168]{1,0:T(8,128)(2,1)S(1)}, u32[]{:S(2)}, u32[]{:S(2)}) %collective-permute-start.29) | collective-permute-done | bytes 114720 | tf_op jit(solution)/shard_map/ppermute | solution.py:37
  (84 shorter events, 23.5 us)
Async XLA Ops:
  0.6 151.4 %copy-start = (bf16[8,128,512]{2,1,0:T(8,128)(2,1)S(1)}, bf16[8,128,512]{2,1,0:T(8,128)(2,1)}, u32[]{:S(2)}) copy-start(bf16[8,128,512]{2,1,0:T(8,128)(2,1)} %param.14) | copy-start | bytes 3145732
  2.5 6.9 %collective-permute-start.2 = (bf16[8,7296]{1,0:T(8,128)(2,1)}, bf16[8,7296]{1,0:T(8,128)(2,1)S(1)}, u32[]{:S(2)}, u32[]{:S(2)}) collective-permute-start(bf16[8,7296]{1,0:T(8,128)(2,1)} %prepare.1), channel_id=1, source_target_pairs={{0,4},{1,65},{2,6},{3,67},{4,0},{5,69},{6,2},{7,71},{8,12},{9,73},... | collective-permute-start | bytes 350216 | tf_op jit(solution)/shard_map/ppermute | solution.py:37
  6.4 5.3 %collective-permute-start.1 = (bf16[8,7296]{1,0:T(8,128)(2,1)}, bf16[8,7296]{1,0:T(8,128)(2,1)S(1)}, u32[]{:S(2)}, u32[]{:S(2)}) collective-permute-start(bf16[8,7296]{1,0:T(8,128)(2,1)} %prepare.1), channel_id=1, source_target_pairs={{0,6},{1,97},{2,0},{3,99},{4,2},{5,101},{6,4},{7,103},{8,14},{9,10... | collective-permute-start | bytes 350216 | tf_op jit(solution)/shard_map/ppermute | solution.py:37
  7.1 6.2 %collective-permute-start = (bf16[8,7296]{1,0:T(8,128)(2,1)}, bf16[8,7296]{1,0:T(8,128)(2,1)S(1)}, u32[]{:S(2)}, u32[]{:S(2)}) collective-permute-start(bf16[8,7296]{1,0:T(8,128)(2,1)} %prepare.1), channel_id=1, source_target_pairs={{0,2},{1,33},{2,4},{3,35},{4,6},{5,37},{6,0},{7,39},{8,10},{9,41},... | collective-permute-start | bytes 350216 | tf_op jit(solution)/shard_map/ppermute | solution.py:37
  14.2 9.8 %collective-permute-start.4 = (bf16[32,7296]{1,0:T(8,128)(2,1)S(1)}, bf16[32,7296]{1,0:T(8,128)(2,1)S(1)}, u32[]{:S(2)}, u32[]{:S(2)}) collective-permute-start(bf16[32,7296]{1,0:T(8,128)(2,1)S(1)} %pad_maximum_fusion.2), channel_id=1, source_target_pairs={{0,24},{1,7},{2,26},{3,1},{4,28},{5,3},{6,30},{7,5},{8,0},{9,15},{... | collective-permute-start | bytes 1400840 | tf_op jit(solution)/shard_map/ppermute | solution.py:37
  15.1 9.1 %collective-permute-start.3 = (bf16[32,7296]{1,0:T(8,128)(2,1)S(1)}, bf16[32,7296]{1,0:T(8,128)(2,1)S(1)}, u32[]{:S(2)}, u32[]{:S(2)}) collective-permute-start(bf16[32,7296]{1,0:T(8,128)(2,1)S(1)} %pad_maximum_fusion.2), channel_id=1, source_target_pairs={{0,8},{1,3},{2,10},{3,5},{4,12},{5,7},{6,14},{7,1},{8,16},{9,11},{... | collective-permute-start | bytes 1400840 | tf_op jit(solution)/shard_map/ppermute | solution.py:37
  24.1 7.3 %collective-permute-start.6 = (bf16[16,7296]{1,0:T(8,128)(2,1)S(1)}, bf16[16,7296]{1,0:T(8,128)(2,1)S(1)}, u32[]{:S(2)}, u32[]{:S(2)}) collective-permute-start(bf16[16,7296]{1,0:T(8,128)(2,1)S(1)} %slice.83), channel_id=1, source_target_pairs={{0,24},{1,7},{2,26},{3,1},{4,28},{5,3},{6,30},{7,5},{8,0},{9,15},{... | collective-permute-start | bytes 700424 | tf_op jit(solution)/shard_map/ppermute | solution.py:37
  24.2 6.9 %collective-permute-start.5 = (bf16[16,7296]{1,0:T(8,128)(2,1)S(1)}, bf16[16,7296]{1,0:T(8,128)(2,1)S(1)}, u32[]{:S(2)}, u32[]{:S(2)}) collective-permute-start(bf16[16,7296]{1,0:T(8,128)(2,1)S(1)} %slice.82), channel_id=1, source_target_pairs={{0,8},{1,3},{2,10},{3,5},{4,12},{5,7},{6,14},{7,1},{8,16},{9,11},{... | collective-permute-start | bytes 700424 | tf_op jit(solution)/shard_map/ppermute | solution.py:37
  31.5 7.4 %collective-permute-start.9 = (bf16[128,7296]{1,0:T(8,128)(2,1)S(1)}, bf16[128,7296]{1,0:T(8,128)(2,1)}, u32[]{:S(2)}, u32[]{:S(2)}) collective-permute-start(bf16[128,7296]{1,0:T(8,128)(2,1)S(1)} %constant_dynamic-update-slice_fusion.refs_0_.refs_2_), channel_id=1, source_target_pairs={{0,1},{1,0},{2,3},{3,2},{4,5},{5,4},{6,7},{7,6},{8,9},{9,8},{10,11... | collective-permute-start | bytes 5603336 | tf_op jit(solution)/shard_map/ppermute | solution.py:41
  46.4 4.0 %collective-permute-start.10 = (bf16[128,7168]{1,0:T(8,128)(2,1)S(1)}, bf16[128,7168]{1,0:T(8,128)(2,1)S(1)}, u32[]{:S(2)}, u32[]{:S(2)}) collective-permute-start(bf16[128,7168]{1,0:T(8,128)(2,1)S(1)} %outputs.6), channel_id=1, source_target_pairs={{0,1},{1,0},{2,3},{3,2},{4,5},{5,4},{6,7},{7,6},{8,9},{9,8},{10,11... | collective-permute-start | bytes 5505032 | tf_op jit(solution)/shard_map/ppermute | solution.py:41
  47.0 24.8 %collective-permute-start.8 = (bf16[128,7296]{1,0:T(8,128)(2,1)S(1)}, bf16[128,7296]{1,0:T(8,128)(2,1)S(1)}, u32[]{:S(2)}, u32[]{:S(2)}) collective-permute-start(bf16[128,7296]{1,0:T(8,128)(2,1)S(1)} %constant_dynamic-update-slice_fusion.refs_0_.refs_2_), channel_id=1, source_target_pairs={{0,96},{1,25},{2,98},{3,27},{4,100},{5,29},{6,102},{7,31},{8,104},... | collective-permute-start | bytes 5603336 | tf_op jit(solution)/shard_map/ppermute | solution.py:37
  47.8 23.9 %collective-permute-start.7 = (bf16[128,7296]{1,0:T(8,128)(2,1)S(1)}, bf16[128,7296]{1,0:T(8,128)(2,1)S(1)}, u32[]{:S(2)}, u32[]{:S(2)}) collective-permute-start(bf16[128,7296]{1,0:T(8,128)(2,1)S(1)} %constant_dynamic-update-slice_fusion.refs_0_.refs_2_), channel_id=1, source_target_pairs={{0,32},{1,9},{2,34},{3,11},{4,36},{5,13},{6,38},{7,15},{8,40},{9,1... | collective-permute-start | bytes 5603336 | tf_op jit(solution)/shard_map/ppermute | solution.py:37
  71.7 9.0 %collective-permute-start.13 = (bf16[128,7296]{1,0:T(8,128)(2,1)S(1)}, bf16[128,7296]{1,0:T(8,128)(2,1)S(1)}, u32[]{:S(2)}, u32[]{:S(2)}) collective-permute-start(bf16[128,7296]{1,0:T(8,128)(2,1)S(1)} %collective-permute-done.7.refs_0_.refs_2_), channel_id=1, source_target_pairs={{0,1},{1,0},{2,3},{3,2},{4,5},{5,4},{6,7},{7,6},{8,9},{9,8},{10,11... | collective-permute-start | bytes 5603336 | tf_op jit(solution)/shard_map/ppermute | solution.py:41
  71.7 9.0 %collective-permute-start.14 = (bf16[128,7296]{1,0:T(8,128)(2,1)S(1)}, bf16[128,7296]{1,0:T(8,128)(2,1)S(1)}, u32[]{:S(2)}, u32[]{:S(2)}) collective-permute-start(bf16[128,7296]{1,0:T(8,128)(2,1)S(1)} %collective-permute-done.8.refs_1_.refs_3_), channel_id=1, source_target_pairs={{0,1},{1,0},{2,3},{3,2},{4,5},{5,4},{6,7},{7,6},{8,9},{9,8},{10,11... | collective-permute-start | bytes 5603336 | tf_op jit(solution)/shard_map/ppermute | solution.py:41
  72.4 14.9 %collective-permute-start.12 = (bf16[64,7296]{1,0:T(8,128)(2,1)S(1)}, bf16[64,7296]{1,0:T(8,128)(2,1)S(1)}, u32[]{:S(2)}, u32[]{:S(2)}) collective-permute-start(bf16[64,7296]{1,0:T(8,128)(2,1)S(1)} %slice.66), channel_id=1, source_target_pairs={{0,96},{1,25},{2,98},{3,27},{4,100},{5,29},{6,102},{7,31},{8,104},... | collective-permute-start | bytes 2801672 | tf_op jit(solution)/shard_map/ppermute | solution.py:37
  72.6 14.6 %collective-permute-start.11 = (bf16[64,7296]{1,0:T(8,128)(2,1)S(1)}, bf16[64,7296]{1,0:T(8,128)(2,1)S(1)}, u32[]{:S(2)}, u32[]{:S(2)}) collective-permute-start(bf16[64,7296]{1,0:T(8,128)(2,1)S(1)} %slice.65), channel_id=1, source_target_pairs={{0,32},{1,9},{2,34},{3,11},{4,36},{5,13},{6,38},{7,15},{8,40},{9,1... | collective-permute-start | bytes 2801672 | tf_op jit(solution)/shard_map/ppermute | solution.py:37
  87.2 3.4 %collective-permute-start.15 = (bf16[64,7296]{1,0:T(8,128)(2,1)S(1)}, bf16[64,7296]{1,0:T(8,128)(2,1)S(1)}, u32[]{:S(2)}, u32[]{:S(2)}) collective-permute-start(bf16[64,7296]{1,0:T(8,128)(2,1)S(1)} %collective-permute-done.11.refs_0_.refs_4_), channel_id=1, source_target_pairs={{0,1},{1,0},{2,3},{3,2},{4,5},{5,4},{6,7},{7,6},{8,9},{9,8},{10,11... | collective-permute-start | bytes 2801672 | tf_op jit(solution)/shard_map/ppermute | solution.py:41
  87.2 3.8 %collective-permute-start.16 = (bf16[64,7296]{1,0:T(8,128)(2,1)S(1)}, bf16[64,7296]{1,0:T(8,128)(2,1)S(1)}, u32[]{:S(2)}, u32[]{:S(2)}) collective-permute-start(bf16[64,7296]{1,0:T(8,128)(2,1)S(1)} %collective-permute-done.12.refs_1_.refs_5_), channel_id=1, source_target_pairs={{0,1},{1,0},{2,3},{3,2},{4,5},{5,4},{6,7},{7,6},{8,9},{9,8},{10,11... | collective-permute-start | bytes 2801672 | tf_op jit(solution)/shard_map/ppermute | solution.py:41
  91.1 7.4 %collective-permute-start.17 = (bf16[256,7168]{1,0:T(8,128)(2,1)S(1)}, bf16[256,7168]{1,0:T(8,128)(2,1)S(1)}, u32[]{:S(2)}, u32[]{:S(2)}) collective-permute-start(bf16[256,7168]{1,0:T(8,128)(2,1)S(1)} %outputs.8), channel_id=1, source_target_pairs={{0,1},{1,0},{2,3},{3,2},{4,5},{5,4},{6,7},{7,6},{8,9},{9,8},{10,11... | collective-permute-start | bytes 11010056 | tf_op jit(solution)/shard_map/ppermute | solution.py:41
  98.1 3.9 %collective-permute-start.18 = (bf16[128,7168]{1,0:T(8,128)(2,1)S(1)}, bf16[128,7168]{1,0:T(8,128)(2,1)S(1)}, u32[]{:S(2)}, u32[]{:S(2)}) collective-permute-start(bf16[128,7168]{1,0:T(8,128)(2,1)S(1)} %outputs.9), channel_id=1, source_target_pairs={{0,1},{1,0},{2,3},{3,2},{4,5},{5,4},{6,7},{7,6},{8,9},{9,8},{10,11... | collective-permute-start | bytes 5505032 | tf_op jit(solution)/shard_map/ppermute | solution.py:41
  103.9 14.5 %collective-permute-start.21 = (bf16[64,7168]{1,0:T(8,128)(2,1)S(1)}, bf16[64,7168]{1,0:T(8,128)(2,1)S(1)}, u32[]{:S(2)}, u32[]{:S(2)}) collective-permute-start(bf16[64,7168]{1,0:T(8,128)(2,1)S(1)} %get-tuple-element.49), channel_id=1, source_target_pairs={{0,32},{1,9},{2,34},{3,11},{4,36},{5,13},{6,38},{7,15},{8,40},{9,1... | collective-permute-start | bytes 2752520 | tf_op jit(solution)/shard_map/ppermute | solution.py:37
  107.6 14.9 %collective-permute-start.19 = (bf16[64,7168]{1,0:T(8,128)(2,1)S(1)}, bf16[64,7168]{1,0:T(8,128)(2,1)S(1)}, u32[]{:S(2)}, u32[]{:S(2)}) collective-permute-start(bf16[64,7168]{1,0:T(8,128)(2,1)S(1)} %get-tuple-element.47), channel_id=1, source_target_pairs={{0,96},{1,25},{2,98},{3,27},{4,100},{5,29},{6,102},{7,31},{8,104},... | collective-permute-start | bytes 2752520 | tf_op jit(solution)/shard_map/ppermute | solution.py:37
  118.7 24.5 %collective-permute-start.22 = (bf16[128,7168]{1,0:T(8,128)(2,1)S(1)}, bf16[128,7168]{1,0:T(8,128)(2,1)S(1)}, u32[]{:S(2)}, u32[]{:S(2)}) collective-permute-start(bf16[128,7168]{1,0:T(8,128)(2,1)S(1)} %pad_maximum_fusion.1), channel_id=1, source_target_pairs={{0,32},{1,9},{2,34},{3,11},{4,36},{5,13},{6,38},{7,15},{8,40},{9,1... | collective-permute-start | bytes 5505032 | tf_op jit(solution)/shard_map/ppermute | solution.py:37
  122.9 24.7 %collective-permute-start.20 = (bf16[128,7168]{1,0:T(8,128)(2,1)S(1)}, bf16[128,7168]{1,0:T(8,128)(2,1)S(1)}, u32[]{:S(2)}, u32[]{:S(2)}) collective-permute-start(bf16[128,7168]{1,0:T(8,128)(2,1)S(1)} %pad_maximum_fusion), channel_id=1, source_target_pairs={{0,96},{1,25},{2,98},{3,27},{4,100},{5,29},{6,102},{7,31},{8,104},... | collective-permute-start | bytes 5505032 | tf_op jit(solution)/shard_map/ppermute | solution.py:37
  148.5 7.5 %collective-permute-start.23 = (bf16[16,7168]{1,0:T(8,128)(2,1)S(1)}, bf16[16,7168]{1,0:T(8,128)(2,1)S(1)}, u32[]{:S(2)}, u32[]{:S(2)}) collective-permute-start(bf16[16,7168]{1,0:T(8,128)(2,1)S(1)} %get-tuple-element.52), channel_id=1, source_target_pairs={{0,24},{1,7},{2,26},{3,1},{4,28},{5,3},{6,30},{7,5},{8,0},{9,15},{... | collective-permute-start | bytes 688136 | tf_op jit(solution)/shard_map/ppermute | solution.py:37
  148.6 7.4 %collective-permute-start.25 = (bf16[16,7168]{1,0:T(8,128)(2,1)S(1)}, bf16[16,7168]{1,0:T(8,128)(2,1)S(1)}, u32[]{:S(2)}, u32[]{:S(2)}) collective-permute-start(bf16[16,7168]{1,0:T(8,128)(2,1)S(1)} %get-tuple-element.53), channel_id=1, source_target_pairs={{0,8},{1,3},{2,10},{3,5},{4,12},{5,7},{6,14},{7,1},{8,16},{9,11},{... | collective-permute-start | bytes 688136 | tf_op jit(solution)/shard_map/ppermute | solution.py:37
  156.1 9.4 %collective-permute-start.26 = (bf16[32,7168]{1,0:T(8,128)(2,1)S(1)}, bf16[32,7168]{1,0:T(8,128)(2,1)S(1)}, u32[]{:S(2)}, u32[]{:S(2)}) collective-permute-start(bf16[32,7168]{1,0:T(8,128)(2,1)S(1)} %pad_maximum_fusion.4), channel_id=1, source_target_pairs={{0,8},{1,3},{2,10},{3,5},{4,12},{5,7},{6,14},{7,1},{8,16},{9,11},{... | collective-permute-start | bytes 1376264 | tf_op jit(solution)/shard_map/ppermute | solution.py:37
  159.5 9.8 %collective-permute-start.24 = (bf16[32,7168]{1,0:T(8,128)(2,1)S(1)}, bf16[32,7168]{1,0:T(8,128)(2,1)S(1)}, u32[]{:S(2)}, u32[]{:S(2)}) collective-permute-start(bf16[32,7168]{1,0:T(8,128)(2,1)S(1)} %pad_maximum_fusion.3), channel_id=1, source_target_pairs={{0,24},{1,7},{2,26},{3,1},{4,28},{5,3},{6,30},{7,5},{8,0},{9,15},{... | collective-permute-start | bytes 1376264 | tf_op jit(solution)/shard_map/ppermute | solution.py:37
  169.4 8.6 %copy-start.2 = (bf16[8,7168]{1,0:T(8,128)(2,1)S(1)}, bf16[8,7168]{1,0:T(8,128)(2,1)}, u32[]{:S(2)}) copy-start(bf16[8,7168]{1,0:T(8,128)(2,1)} %stream_ref.1) | copy-start | bytes 344068
  169.5 4.9 %collective-permute-start.27 = (bf16[8,7168]{1,0:T(8,128)(2,1)S(1)}, bf16[8,7168]{1,0:T(8,128)(2,1)S(1)}, u32[]{:S(2)}, u32[]{:S(2)}) collective-permute-start(bf16[8,7168]{1,0:T(8,128)(2,1)S(1)} %get-tuple-element.56), channel_id=1, source_target_pairs={{0,6},{1,97},{2,0},{3,99},{4,2},{5,101},{6,4},{7,103},{8,14},{9,10... | collective-permute-start | bytes 344072 | tf_op jit(solution)/shard_map/ppermute | solution.py:37
  170.6 6.3 %collective-permute-start.29 = (bf16[8,7168]{1,0:T(8,128)(2,1)S(1)}, bf16[8,7168]{1,0:T(8,128)(2,1)S(1)}, u32[]{:S(2)}, u32[]{:S(2)}) collective-permute-start(bf16[8,7168]{1,0:T(8,128)(2,1)S(1)} %get-tuple-element.57), channel_id=1, source_target_pairs={{0,4},{1,65},{2,6},{3,67},{4,0},{5,69},{6,2},{7,71},{8,12},{9,73},... | collective-permute-start | bytes 344072 | tf_op jit(solution)/shard_map/ppermute | solution.py:37
  171.7 6.4 %collective-permute-start.28 = (bf16[8,7168]{1,0:T(8,128)(2,1)S(1)}, bf16[8,7168]{1,0:T(8,128)(2,1)S(1)}, u32[]{:S(2)}, u32[]{:S(2)}) collective-permute-start(bf16[8,7168]{1,0:T(8,128)(2,1)S(1)} %get-tuple-element.58), channel_id=1, source_target_pairs={{0,2},{1,33},{2,4},{3,35},{4,6},{5,37},{6,0},{7,39},{8,10},{9,41},... | collective-permute-start | bytes 344072 | tf_op jit(solution)/shard_map/ppermute | solution.py:37
  (4 other events, 25.2 us)
where the time goes:
time: 179 us
  waiting for transfers between devices  88.1 us (49%)
  Pallas kernels  43 us (24%)
  starting transfers between devices  38.9 us (22%)
  other arithmetic  3.76 us (2%)
  matrix products  2.42 us (1%)
    ppermute x22, waiting for transfers between devices, move(): return lax.ppermute(block, TORUS, torus_pairs(phase, step))  87.3 us
    ppermute x22, starting transfers between devices, move(): return lax.ppermute(block, TORUS, torus_pairs(phase, step))  36.7 us
    pallas_call x4, Pallas kernels, hidden_of(): pl.pallas_call(kernel, grid=(steps,), in_specs=[pl.BlockSpec(memory_space...  20.2 us
    pallas_call x6, Pallas kernels, outputs_of(): pl.pallas_call(kernel, grid=(steps,), in_specs=specs, out_specs=[pl.Block...  13.6 us
    pallas_call x1, Pallas kernels, resident(): pl.pallas_call(kernel, in_specs=[pl.BlockSpec(memory_space=pltpu.HBM)] *...  7.29 us
  transfers between devices with their start and end apart: 30, of which 19 were waited for; matrix products, arithmetic and copies ran while one was open for 3% of the time, Pallas kernels for 18%

commit v1 on v0

--- a/solution.py
+++ b/solution.py
@@ -14,7 +14,7 @@
 score_scale = 192.0 ** (-0.5)
 norm_eps = 1e-06
 meta_lanes = 128
-vmem_share = 16 << 20
+vmem_share = 8 << 20
 
 PHASE_AXES = ((2, 1, 0), (0, 2, 1))
 
@@ -62,24 +62,43 @@
     return widen(own) + widen(got[0]) + widen(got[1]) + widen(got[2])
 
 
-def spread_ring(block, phase):
-    half = block.shape[0] // 2
-    behind = move(block, phase, 1)
-    ahead = move(block, phase, -1)
-    across_a = move(behind[:half], phase, 1)
-    across_b = move(ahead[half:], phase, -1)
-    return [block, behind, ahead, across_a, across_b]
-
-
-def fold_ring(own, behind, ahead, across_a, across_b, phase):
-    half = own.shape[0] // 2
-    via_a = move(narrow(across_a), phase, -1)
-    via_b = move(narrow(across_b), phase, 1)
-    behind = jnp.concatenate([narrow(widen(behind[:half]) + widen(via_a)), narrow(behind[half:])])
-    ahead = jnp.concatenate([narrow(ahead[:half]), narrow(widen(ahead[half:]) + widen(via_b))])
-    got_a = move(behind, phase, -1)
-    got_b = move(ahead, phase, 1)
-    return widen(own) + widen(got_a) + widen(got_b)
+def pack(blocks):
+    count = len(blocks)
+    sizes = [b.shape[0] for b in blocks]
+
+    def kernel(*refs):
+        out_ref = refs[-1]
+        at = 0
+        for ref, n in zip(refs[:count], sizes):
+            out_ref[at : at + n] = ref[...]
+            at += n
+
+    return pl.pallas_call(
+        kernel,
+        in_specs=[pl.BlockSpec(memory_space=pltpu.VMEM)] * count,
+        out_shape=jax.ShapeDtypeStruct((sum(sizes), blocks[0].shape[1]), blocks[0].dtype),
+        compiler_params=pltpu.CompilerParams(vmem_limit_bytes=vmem_share),
+        name="pack",
+    )(*blocks)
+
+
+def merge(block, via, at, via_at, count):
+    rows = block.shape[0]
+
+    def kernel(block_ref, via_ref, out_ref):
+        if at:
+            out_ref[:at] = block_ref[:at]
+        added = widen(block_ref[at : at + count]) + widen(via_ref[via_at : via_at + count])
+        out_ref[at : at + count] = narrow(added)
+        if at + count < rows:
+            out_ref[at + count :] = block_ref[at + count :]
+
+    return pl.pallas_call(
+        kernel,
+        out_shape=jax.ShapeDtypeStruct(block.shape, block.dtype),
+        compiler_params=pltpu.CompilerParams(vmem_limit_bytes=vmem_share),
+        name="merge",
+    )(block, via)
 
 
 def prepare(stream, norm_gain, expert_ids, route_weights):
@@ -104,28 +123,79 @@
     )(stream, norm_gain.reshape(1, -1), expert_ids, route_weights)
 
 
-def resident(*arrays):
-    count = len(arrays)
-
-    def kernel(*refs):
-        sources, targets, sems = refs[:count], refs[count : 2 * count], refs[2 * count]
-        copies = [
-            pltpu.make_async_copy(sources[i], targets[i], sems.at[i]) for i in range(count)
-        ]
-        for copy in copies:
-            copy.start()
-        for copy in copies:
-            copy.wait()
-
-    return pl.pallas_call(
-        kernel,
-        in_specs=[pl.BlockSpec(memory_space=pltpu.HBM)] * count,
-        out_specs=[pl.BlockSpec(memory_space=pltpu.VMEM)] * count,
-        out_shape=[pltpu.VMEM(a.shape, a.dtype) for a in arrays],
-        scratch_shapes=[pltpu.SemaphoreType.DMA((count,))],
-        compiler_params=pltpu.CompilerParams(vmem_limit_bytes=vmem_share),
-        name="resident",
-    )(*[pltpu.with_memory_space_constraint(a, pltpu.HBM) for a in arrays])
+def finish(acc_ref, meta, first, out_ref, local_count, units):
+    lane = lax.broadcasted_iota(jnp.int32, meta.shape, 1)
+    for e in range(local_count):
+        mine = jnp.where(lane == first + e, widen(meta), 0.0)
+        share = jnp.sum(mine, axis=1, keepdims=True)
+        act = jax.nn.silu(acc_ref[2 * e]) * acc_ref[2 * e + 1] * share
+        out_ref[:, e * units : (e + 1) * units] = narrow(act)
+
+
+def first_hidden(blocks, w_gate, w_up, w_down, first_expert):
+    local_count, width, units = w_gate.shape
+    steps = 7
+    tile = width // steps
+    total = sum(b.shape[0] for b in blocks)
+    count = len(blocks)
+
+    def kernel(first_ref, *refs):
+        rows_refs = refs[:count]
+        sources = refs[count : count + 3]
+        out_ref, gate_ref, up_ref, down_ref, acc_ref, sems, down_sem = refs[count + 3 :]
+
+        def piece(k, which):
+            here = pl.ds(k * tile, tile)
+            target = (gate_ref, up_ref)[which]
+            return pltpu.make_async_copy(
+                sources[which].at[:, here, :], target.at[:, here, :], sems.at[k, which]
+            )
+
+        for k in range(steps):
+            piece(k, 0).start()
+            piece(k, 1).start()
+        last = pltpu.make_async_copy(sources[2], down_ref, down_sem)
+        last.start()
+        for k in range(steps):
+            here = slice(k * tile, (k + 1) * tile)
+            rows = jnp.concatenate([r[:, here] for r in rows_refs], axis=0)
+            for which, ref in enumerate((gate_ref, up_ref)):
+                piece(k, which).wait()
+                for e in range(local_count):
+                    part = jnp.dot(rows, ref[e, here, :], preferred_element_type=jnp.float32)
+                    if k:
+                        part = part + acc_ref[2 * e + which]
+                    acc_ref[2 * e + which] = part
+        meta = jnp.concatenate([r[:, width:] for r in rows_refs], axis=0)
+        finish(acc_ref, meta, first_ref[0], out_ref, local_count, units)
+        last.wait()
+
+    weights = (w_gate, w_up, w_down)
+    return pl.pallas_call(
+        kernel,
+        in_specs=[pl.BlockSpec(memory_space=pltpu.SMEM)]
+        + [pl.BlockSpec(memory_space=pltpu.VMEM)] * count
+        + [pl.BlockSpec(memory_space=pltpu.HBM)] * 3,
+        out_specs=[pl.BlockSpec(memory_space=pltpu.VMEM)] * 4,
+        out_shape=[jax.ShapeDtypeStruct((total, local_count * units), jnp.bfloat16)]
+        + [pltpu.VMEM(w.shape, w.dtype) for w in weights],
+        scratch_shapes=[
+            pltpu.VMEM((2 * local_count, total, units), jnp.float32),
+            pltpu.SemaphoreType.DMA((steps, 2)),
+            pltpu.SemaphoreType.DMA,
+        ],
+        compiler_params=pltpu.CompilerParams(vmem_limit_bytes=vmem_share + (4 << 20)),
+        cost_estimate=pl.CostEstimate(
+            flops=4 * total * width * units * local_count,
+            transcendentals=total * units * local_count,
+            bytes_accessed=6 * width * units * local_count,
+        ),
+        name="first_hidden",
+    )(
+        first_expert,
+        *blocks,
+        *[pltpu.with_memory_space_constraint(w, pltpu.HBM) for w in weights],
+    )
 
 
 def hidden_of(blocks, w_gate, w_up, first_expert):
@@ -154,13 +224,8 @@
 
         @pl.when(step == steps - 1)
         def _():
-            meta = widen(jnp.concatenate([r[...] for r in meta_refs], axis=0))
-            lane = lax.broadcasted_iota(jnp.int32, meta.shape, 1)
-            for e in range(local_count):
-                mine = jnp.where(lane == first_ref[0] + e, meta, 0.0)
-                share = jnp.sum(mine, axis=1, keepdims=True)
-                act = jax.nn.silu(acc_ref[2 * e]) * acc_ref[2 * e + 1] * share
-                out_ref[:, e * units : (e + 1) * units] = narrow(act)
+            meta = jnp.concatenate([r[...] for r in meta_refs], axis=0)
+            finish(acc_ref, meta, first_ref[0], out_ref, local_count, units)
 
     return pl.pallas_call(
         kernel,
@@ -271,53 +336,68 @@
     payload = prepare(stream, norm_gain, expert_ids, route_weights)
 
     line = jnp.concatenate(spread_direct(payload, 0))
-    plane = jnp.concatenate(spread_ring(line, 1))
-    block = plane.shape[0]
-    half = block // 2
-    behind = move(plane, 2, 1)
-    ahead = move(plane, 2, -1)
-    plane_2 = swap(plane)
-    w_gate, w_up, down = resident(w_gate, w_up, w_down)
-    hid_own = hidden_of([plane, plane_2], w_gate, w_up, first_expert)
+    size = line.shape[0]
+    half = size // 2
+    near_rows = 3 * size
+    near_half = near_rows // 2
+    block = 4 * size
+
+    line_behind = move(line, 1, 1)
+    line_ahead = move(line, 1, -1)
+    line_far_a = move(line_behind[:half], 1, 1)
+    line_far_b = move(line_ahead[half:], 1, -1)
+    own_a = pack([line, line_behind, line_ahead])
+    behind_a = move(own_a, 2, 1)
+    ahead_a = move(own_a, 2, -1)
+    own_b = pack([line_far_a, line_far_b])
+    behind_b = move(own_b, 2, 1)
+    ahead_b = move(own_b, 2, -1)
+    own_a2 = swap(own_a)
+    own_b2 = swap(own_b)
+    hid_own, w_gate, w_up, down = first_hidden(
+        [own_a, own_b, own_a2, own_b2], w_gate, w_up, w_down, first_expert
+    )
+    far_wide_a = move(behind_a[:near_half], 2, 1)
+    far_wide_b = move(ahead_a[near_half:], 2, -1)
+    behind_a2 = swap(behind_a)
+    ahead_a2 = swap(ahead_a)
+    far_slim_a = move(behind_b[:half], 2, 1)
+    far_slim_b = move(ahead_b[half:], 2, -1)
+    behind_b2 = swap(behind_b)
+    ahead_b2 = swap(ahead_b)
+    hid_near = hidden_of([behind_a, behind_b, ahead_a, ahead_b], w_gate, w_up, first_expert)
+    behind_a2, hid_near = after((behind_a2, hid_near))
+    hid_near_2 = hidden_of([behind_a2, behind_b2, ahead_a2, ahead_b2], w_gate, w_up, first_expert)
+    far = [far_wide_a, far_slim_a, far_wide_b, far_slim_b]
+    far_2 = [swap(f) for f in far]
+    (near_2,) = outputs_of(hid_near_2, 0, [2 * block], down)
+    *far_2, near_2 = after((*far_2, near_2))
+    near_got = swap(near_2)
+    hid_far = hidden_of(far + far_2, w_gate, w_up, first_expert)
+    (far_part,) = outputs_of(hid_far, 1, [block], down)
+    hid_near, far_part = after((hid_near, far_part))
+    far_got = swap(far_part)
+    near = outputs_of(hid_near, 0, [near_rows, size, near_rows, size], down, near_got)
+    hid_far, *near = after((hid_far, *near))
+    far_a, far_b = outputs_of(hid_far, 0, [block // 2, block // 2], down, far_got)
+
+    via_a = move(far_a, 2, -1)
+    via_b = move(far_b, 2, 1)
     (own_2,) = outputs_of(hid_own, 1, [block], down)
     own_got = swap(own_2)
-    (mine,) = outputs_of(hid_own, 0, [block], down, own_got)
-
-    behind, ahead, mine = after((behind, ahead, mine))
-    across_a = move(behind[:half], 2, 1)
-    across_b = move(ahead[half:], 2, -1)
-    behind_2 = swap(behind)
-    ahead_2 = swap(ahead)
-    hid_near = hidden_of([behind, ahead], w_gate, w_up, first_expert)
-    behind_2, ahead_2, hid_near = after((behind_2, ahead_2, hid_near))
-    hid_near_2 = hidden_of([behind_2, ahead_2], w_gate, w_up, first_expert)
-
-    across_a, across_b, hid_near_2 = after((across_a, across_b, hid_near_2))
-    across_a2 = swap(across_a)
-    across_b2 = swap(across_b)
-    (near_2,) = outputs_of(hid_near_2, 0, [2 * block], down)
-    across_a2, across_b2, near_2 = after((across_a2, across_b2, near_2))
-    near_got = swap(near_2)
-    hid_far = hidden_of([across_a, across_b, across_a2, across_b2], w_gate, w_up, first_expert)
-    (far_2,) = outputs_of(hid_far, 1, [block], down)
-    hid_near, far_2 = after((hid_near, far_2))
-    far_got = swap(far_2)
-    near_a, near_b = outputs_of(hid_near, 0, [block, block], down, near_got)
-    hid_far, near_a, near_b = after((hid_far, near_a, near_b))
-    far_a, far_b = outputs_of(hid_far, 0, [half, half], down, far_got)
-
-    plane_sum = fold_ring(mine, near_a, near_b, far_a, far_b, 2)
-    quarter = block // 4
-    plane_sum = narrow(plane_sum)
-    line_sum = fold_ring(
-        plane_sum[:quarter],
-        plane_sum[quarter : 2 * quarter],
-        plane_sum[2 * quarter : 3 * quarter],
-        plane_sum[3 * quarter : 3 * quarter + quarter // 2],
-        plane_sum[3 * quarter + quarter // 2 :],
-        1,
-    )
-    line_sum = narrow(line_sum)
+    mine_a, mine_b = outputs_of(hid_own, 0, [near_rows, size], down, own_got)
+    behind_a, behind_b, ahead_a, ahead_b = near
+    slim_got_a = move(merge(behind_b, via_a, 0, near_half, half), 2, -1)
+    slim_got_b = move(merge(ahead_b, via_b, half, near_half, half), 2, 1)
+    wide_got_a = move(merge(behind_a, via_a, 0, 0, near_half), 2, -1)
+    wide_got_b = move(merge(ahead_a, via_b, near_half, 0, near_half), 2, 1)
+    slim = narrow(widen(mine_b) + widen(slim_got_a) + widen(slim_got_b))
+    line_via_a = move(slim[:half], 1, -1)
+    line_via_b = move(slim[half:], 1, 1)
+    wide = narrow(widen(mine_a) + widen(wide_got_a) + widen(wide_got_b))
+    line_got_a = move(merge(wide[size : 2 * size], line_via_a, 0, 0, half), 1, -1)
+    line_got_b = move(merge(wide[2 * size :], line_via_b, half, 0, half), 1, 1)
+    line_sum = narrow(widen(wide[:size]) + widen(line_got_a) + widen(line_got_b))
     expert_sum = fold_direct(
         line_sum[:row_count],
         line_sum[row_count : 2 * row_count],

time: 179 us -> 181 us (1.011)
  the two profiles are of different devices: /device:TPU:30 before, /device:TPU:1 now
where the time goes in v1:
time: 181 us; the launch traced here: 178 us
  waiting for transfers between devices  66.6 us (37%)
  starting transfers between devices  55.8 us (31%)
  Pallas kernels  43.7 us (24%)
  local copies, waits for them, and re-layouts  5.96 us (3%)
  other arithmetic  2.78 us (2%)
  matrix products  2.44 us (1%)
    ppermute x28, waiting for transfers between devices, move(): return lax.ppermute(block, TORUS, torus_pairs(phase, step))  66.6 us
    ppermute x28, starting transfers between devices, move(): return lax.ppermute(block, TORUS, torus_pairs(phase, step))  39.6 us
    pallas_call x3, Pallas kernels, hidden_of(): pl.pallas_call(kernel, grid=(steps,), in_specs=[pl.BlockSpec(memory_space...  17 us
    ppermute x13, starting transfers between devices, swap(): return lax.ppermute(block, 'ep_2', [(0, 1), (1, 0)])  16.2 us
    pallas_call x6, Pallas kernels, outputs_of(): pl.pallas_call(kernel, grid=(steps,), in_specs=specs, out_specs=[pl.Block...  13.7 us
    pallas_call x1, Pallas kernels, first_hidden(): pl.pallas_call(kernel, in_specs=[pl.BlockSpec(memory_space=pltpu.SMEM)] +...  9.27 us
  transfers between devices with their start and end apart: 41, of which 15 were waited for; matrix products, arithmetic and copies ran while one was open for 4% of the time, Pallas kernels for 23%

profile of v1, /device:TPU:1, one launch (start us, length us, event | category | flops | bytes accessed | tf_op | source)
XLA Modules:
  0.0 178.4 jit_solution(14685258536997468858)
XLA Ops:
  2.5 2.0 %collective-permute-start = (bf16[8,7296]{1,0:T(8,128)(2,1)}, bf16[8,7296]{1,0:T(8,128)(2,1)S(1)}, u32[]{:S(2)}, u32[]{:S(2)}) collective-permute-start(bf16[8,7296]{1,0:T(8,128)(2,1)} %prepare.1), channel_id=1, source_target_pairs={{0,2},{1,33},{2,4},{3,35},{4,6},{5,37},{6,0},{7,39},{8,10},{9,41},... | collective-permute-start | bytes 350216 | tf_op jit(solution)/shard_map/ppermute | solution.py:37
  8.4 2.8 %collective-permute-done.2 = bf16[8,7296]{1,0:T(8,128)(2,1)S(1)} collective-permute-done((bf16[8,7296]{1,0:T(8,128)(2,1)}, bf16[8,7296]{1,0:T(8,128)(2,1)S(1)}, u32[]{:S(2)}, u32[]{:S(2)}) %collective-permute-start.2) | collective-permute-done | bytes 116768 | tf_op jit(solution)/shard_map/ppermute | solution.py:37
  14.0 2.5 %collective-permute-start.4 = (bf16[32,7296]{1,0:T(8,128)(2,1)S(1)}, bf16[32,7296]{1,0:T(8,128)(2,1)S(1)}, u32[]{:S(2)}, u32[]{:S(2)}) collective-permute-start(bf16[32,7296]{1,0:T(8,128)(2,1)S(1)} %pad_maximum_fusion.refs_0_), channel_id=1, source_target_pairs={{0,24},{1,7},{2,26},{3,1},{4,28},{5,3},{6,30},{7,5},{8,0},{9,15},{... | collective-permute-start | bytes 1400840 | tf_op jit(solution)/shard_map/ppermute | solution.py:37
  16.5 6.2 %collective-permute-done.3.refs_1_ = bf16[32,7296]{1,0:T(8,128)(2,1)S(1)} collective-permute-done((bf16[32,7296]{1,0:T(8,128)(2,1)S(1)}, bf16[32,7296]{1,0:T(8,128)(2,1)S(1)}, u32[]{:S(2)}, u32[]{:S(2)}) %collective-permute-start.3) | collective-permute-done | bytes 466976 | tf_op jit(solution)/shard_map/ppermute | solution.py:37
  27.6 2.0 %collective-permute-start.6 = (bf16[16,7296]{1,0:T(8,128)(2,1)S(1)}, bf16[16,7296]{1,0:T(8,128)(2,1)S(1)}, u32[]{:S(2)}, u32[]{:S(2)}) collective-permute-start(bf16[16,7296]{1,0:T(8,128)(2,1)S(1)} %slice.61), channel_id=1, source_target_pairs={{0,24},{1,7},{2,26},{3,1},{4,28},{5,3},{6,30},{7,5},{8,0},{9,15},{... | collective-permute-start | bytes 700424 | tf_op jit(solution)/shard_map/ppermute | solution.py:37
  29.5 3.7 %collective-permute-done.5.refs_0_ = bf16[16,7296]{1,0:T(8,128)(2,1)S(1)} collective-permute-done((bf16[16,7296]{1,0:T(8,128)(2,1)S(1)}, bf16[16,7296]{1,0:T(8,128)(2,1)S(1)}, u32[]{:S(2)}, u32[]{:S(2)}) %collective-permute-start.5) | collective-permute-done | bytes 233504 | tf_op jit(solution)/shard_map/ppermute | solution.py:37
  33.4 7.4 %collective-permute-start.7 = (bf16[96,7296]{1,0:T(8,128)(2,1)}, bf16[96,7296]{1,0:T(8,128)(2,1)}, u32[]{:S(2)}, u32[]{:S(2)}) collective-permute-start(bf16[96,7296]{1,0:T(8,128)(2,1)} %pack.2.refs_0_), channel_id=1, source_target_pairs={{0,1},{1,0},{2,3},{3,2},{4,5},{5,4},{6,7},{7,6},{8,9},{9,8},{10,11... | collective-permute-start | bytes 4202504 | tf_op jit(solution)/shard_map/ppermute | solution.py:41
  40.8 9.7 %collective-permute-done.12.refs_1_.refs_5_ = bf16[32,7296]{1,0:T(8,128)(2,1)S(1)} collective-permute-done((bf16[32,7296]{1,0:T(8,128)(2,1)S(1)}, bf16[32,7296]{1,0:T(8,128)(2,1)S(1)}, u32[]{:S(2)}, u32[]{:S(2)}) %collective-permute-start.12) | collective-permute-done | bytes 466976 | tf_op jit(solution)/shard_map/ppermute | solution.py:37
  55.6 2.0 %slice.62 = bf16[48,7296]{1,0:T(8,128)(2,1)} slice(bf16[96,7296]{1,0:T(8,128)(2,1)} %collective-permute-done.10.refs_0_.refs_4_), slice={[0:48], [0:7296]} | slice | bytes 1400832 | tf_op jit(solution)/shard_map/slice | solution.py:360
  58.6 2.2 %collective-permute-start.24 = (bf16[96,7296]{1,0:T(8,128)(2,1)S(1)}, bf16[96,7296]{1,0:T(8,128)(2,1)}, u32[]{:S(2)}, u32[]{:S(2)}) collective-permute-start(bf16[96,7296]{1,0:T(8,128)(2,1)S(1)} %collective-permute-done.14.refs_2_.refs_6_), channel_id=1, source_target_pairs={{0,1},{1,0},{2,3},{3,2},{4,5},{5,4},{6,7},{7,6},{8,9},{9,8},{10,11... | collective-permute-start | bytes 4202504 | tf_op jit(solution)/shard_map/ppermute | solution.py:41
  60.8 2.7 %collective-permute-start.17 = (bf16[16,7296]{1,0:T(8,128)(2,1)S(1)}, bf16[16,7296]{1,0:T(8,128)(2,1)S(1)}, u32[]{:S(2)}, u32[]{:S(2)}) collective-permute-start(bf16[16,7296]{1,0:T(8,128)(2,1)S(1)} %slice.65), channel_id=1, source_target_pairs={{0,96},{1,25},{2,98},{3,27},{4,100},{5,29},{6,102},{7,31},{8,104},... | collective-permute-start | bytes 700424 | tf_op jit(solution)/shard_map/ppermute | solution.py:37
  64.3 2.1 %collective-permute-done.17.refs_3_.refs_11_ = bf16[16,7296]{1,0:T(8,128)(2,1)S(1)} collective-permute-done((bf16[16,7296]{1,0:T(8,128)(2,1)S(1)}, bf16[16,7296]{1,0:T(8,128)(2,1)S(1)}, u32[]{:S(2)}, u32[]{:S(2)}) %collective-permute-start.17) | collective-permute-done | bytes 233504 | tf_op jit(solution)/shard_map/ppermute | solution.py:37
  66.5 3.5 %collective-permute-start.15 = (bf16[48,7296]{1,0:T(8,128)(2,1)}, bf16[48,7296]{1,0:T(8,128)(2,1)}, u32[]{:S(2)}, u32[]{:S(2)}) collective-permute-start(bf16[48,7296]{1,0:T(8,128)(2,1)} %slice.64), channel_id=1, source_target_pairs={{0,96},{1,25},{2,98},{3,27},{4,100},{5,29},{6,102},{7,31},{8,104},... | collective-permute-start | bytes 2101256 | tf_op jit(solution)/shard_map/ppermute | solution.py:37
  71.1 1.9 %collective-permute-start.25 = (bf16[32,7296]{1,0:T(8,128)(2,1)S(1)}, bf16[32,7296]{1,0:T(8,128)(2,1)S(1)}, u32[]{:S(2)}, u32[]{:S(2)}) collective-permute-start(bf16[32,7296]{1,0:T(8,128)(2,1)S(1)} %collective-permute-done.16.refs_3_.refs_7_), channel_id=1, source_target_pairs={{0,1},{1,0},{2,3},{3,2},{4,5},{5,4},{6,7},{7,6},{8,9},{9,8},{10,11... | collective-permute-start | bytes 1400840 | tf_op jit(solution)/shard_map/ppermute | solution.py:41
  75.1 9.3 %first_hidden.1 = (bf16[256,512]{1,0:T(8,128)(2,1)S(1)}, bf16[2,7168,256]{2,1,0:T(8,128)(2,1)S(1)}, bf16[2,7168,256]{2,1,0:T(8,128)(2,1)S(1)}, bf16[2,256,7168]{2,1,0:T(8,128)(2,1)S(1)}) custom-call(s32[1]{0:T(128)} %bitcast.first_ref, bf16[96,7296]{1,0:T(8,128)(2,1)} %pack.2.refs_0_, bf16[32,7296]{1,0:T(8,128)(2,1)S(1)} %copy-done.2, ...), custom_call_target="tpu_custom_call" | custom-call | flops 3758096384 | bytes 22020096 | tf_op jit(solution)/shard_map/first_hidden/pallas_call | solution.py:174
  85.0 5.6 %hidden.3.refs_0_ = bf16[256,512]{1,0:T(8,128)(2,1)S(1)} custom-call(s32[1]{0:T(128)} %bitcast.first_ref, bf16[96,7296]{1,0:T(8,128)(2,1)} %collective-permute-done.10.refs_0_.refs_4_, bf16[32,7296]{1,0:T(8,128)(2,1)S(1)} %collective-permute-done.12.refs_1_.refs_5_, bf16[96,7296]{1,0:T(8,128)(2,1)S(1)} %collective-permute-done.14.refs_2_.refs_6_, ...), custom_call_target="tpu_custom_call" | custom-call | flops 3758096384 | bytes 18350080 | tf_op jit(solution)/shard_map/hidden/pallas_call | solution.py:230
  91.2 5.7 %hidden.4.refs_0_ = bf16[256,512]{1,0:T(8,128)(2,1)S(1)} custom-call(s32[1]{0:T(128)} %bitcast.first_ref, bf16[96,7296]{1,0:T(8,128)(2,1)} %collective-permute-done.22.refs_0_.refs_4_, bf16[32,7296]{1,0:T(8,128)(2,1)S(1)} %collective-permute-done.23.refs_1_.refs_5_, bf16[96,7296]{1,0:T(8,128)(2,1)} %collective-permute-done.24.refs_2_.refs_6_, ...), custom_call_target="tpu_custom_call" | custom-call | flops 3758096384 | bytes 18350080 | tf_op jit(solution)/shard_map/hidden/pallas_call | solution.py:230
  96.9 2.9 %outputs.8 = bf16[256,7168]{1,0:T(8,128)(2,1)S(1)} custom-call(bf16[256,512]{1,0:T(8,128)(2,1)S(1)} %hidden.4.refs_0_, bf16[2,256,7168]{2,1,0:T(8,128)(2,1)S(1)} %get-tuple-element.29.refs_1_), custom_call_target="tpu_custom_call" | custom-call | flops 1879048192 | bytes 14680064 | tf_op jit(solution)/shard_map/outputs/pallas_call | solution.py:285
  100.2 5.7 %hidden.5.refs_0_ = bf16[256,512]{1,0:T(8,128)(2,1)S(1)} custom-call(s32[1]{0:T(128)} %bitcast.first_ref, bf16[48,7296]{1,0:T(8,128)(2,1)} %collective-permute-done.11.refs_0_.refs_8_, bf16[16,7296]{1,0:T(8,128)(2,1)S(1)} %copy-done.4, bf16[48,7296]{1,0:T(8,128)(2,1)} %collective-permute-done.15.refs_2_.refs_10_, bf16[16,7296]{1,0:T(8,128)(2,1)S(1)} %copy-done.6, ...), custom_call_target="tpu_custom_call" | custom-call | flops 3758096384 | bytes 18350080 | tf_op jit(solution)/shard_map/hidden/pallas_call | solution.py:230
  110.2 3.2 %outputs.10 = (bf16[96,7168]{1,0:T(8,128)(2,1)S(1)}, bf16[32,7168]{1,0:T(8,128)(2,1)S(1)}, bf16[96,7168]{1,0:T(8,128)(2,1)S(1)}, bf16[32,7168]{1,0:T(8,128)(2,1)S(1)}) custom-call(bf16[256,512]{1,0:T(8,128)(2,1)S(1)} %hidden.3.refs_0_, bf16[2,256,7168]{2,1,0:T(8,128)(2,1)S(1)} %get-tuple-element.29.refs_1_, bf16[256,7168]{1,0:T(8,128)(2,1)S(1)} %collective-permute-done.26.refs_2_), custom_call_target="tpu_custom_call" | custom-call | flops 1879048192 | bytes 14680064 | tf_op jit(solution)/shard_map/outputs/pallas_call | solution.py:285
  113.4 2.0 %outputs.11 = (bf16[64,7168]{1,0:T(8,128)(2,1)S(1)}, bf16[64,7168]{1,0:T(8,128)(2,1)S(1)}) custom-call(bf16[256,512]{1,0:T(8,128)(2,1)S(1)} %hidden.5.refs_0_, bf16[2,256,7168]{2,1,0:T(8,128)(2,1)S(1)} %get-tuple-element.29.refs_1_, bf16[128,7168]{1,0:T(8,128)(2,1)S(1)} %collective-permute-done.27.refs_2_), custom_call_target="tpu_custom_call" | custom-call | flops 939524096 | bytes 11010048 | tf_op jit(solution)/shard_map/outputs/pallas_call | solution.py:285
  115.5 2.6 %collective-permute-start.28 = (bf16[64,7168]{1,0:T(8,128)(2,1)S(1)}, bf16[64,7168]{1,0:T(8,128)(2,1)S(1)}, u32[]{:S(2)}, u32[]{:S(2)}) collective-permute-start(bf16[64,7168]{1,0:T(8,128)(2,1)S(1)} %get-tuple-element.48), channel_id=1, source_target_pairs={{0,96},{1,25},{2,98},{3,27},{4,100},{5,29},{6,102},{7,31},{8,104},... | collective-permute-start | bytes 2752520 | tf_op jit(solution)/shard_map/ppermute | solution.py:37
  118.1 10.3 %collective-permute-done.28.via_ref = bf16[64,7168]{1,0:T(8,128)(2,1)S(1)} collective-permute-done((bf16[64,7168]{1,0:T(8,128)(2,1)S(1)}, bf16[64,7168]{1,0:T(8,128)(2,1)S(1)}, u32[]{:S(2)}, u32[]{:S(2)}) %collective-permute-start.28) | collective-permute-done | bytes 917536 | tf_op jit(solution)/shard_map/ppermute | solution.py:37
  128.5 3.5 %collective-permute-start.32 = (bf16[32,7168]{1,0:T(8,128)(2,1)S(1)}, bf16[32,7168]{1,0:T(8,128)(2,1)S(1)}, u32[]{:S(2)}, u32[]{:S(2)}) collective-permute-start(bf16[32,7168]{1,0:T(8,128)(2,1)S(1)} %merge.8), channel_id=1, source_target_pairs={{0,96},{1,25},{2,98},{3,27},{4,100},{5,29},{6,102},{7,31},{8,104},... | collective-permute-start | bytes 1376264 | tf_op jit(solution)/shard_map/ppermute | solution.py:37
  132.8 2.0 %outputs.7 = (bf16[96,7168]{1,0:T(8,128)(2,1)S(1)}, bf16[32,7168]{1,0:T(8,128)(2,1)S(1)}) custom-call(bf16[256,512]{1,0:T(8,128)(2,1)S(1)} %get-tuple-element.28.refs_0_, bf16[2,256,7168]{2,1,0:T(8,128)(2,1)S(1)} %get-tuple-element.29.refs_1_, bf16[128,7168]{1,0:T(8,128)(2,1)S(1)} %collective-permute-done.9.refs_2_), custom_call_target="tpu_custom_call" | custom-call | flops 939524096 | bytes 11010048 | tf_op jit(solution)/shard_map/outputs/pallas_call | solution.py:285
  135.0 2.7 %collective-permute-start.29 = (bf16[96,7168]{1,0:T(8,128)(2,1)S(1)}, bf16[96,7168]{1,0:T(8,128)(2,1)S(1)}, u32[]{:S(2)}, u32[]{:S(2)}) collective-permute-start(bf16[96,7168]{1,0:T(8,128)(2,1)S(1)} %merge.6), channel_id=1, source_target_pairs={{0,96},{1,25},{2,98},{3,27},{4,100},{5,29},{6,102},{7,31},{8,104},... | collective-permute-start | bytes 4128776 | tf_op jit(solution)/shard_map/ppermute | solution.py:37
  138.0 3.1 %collective-permute-done.33 = bf16[32,7168]{1,0:T(8,128)(2,1)S(1)} collective-permute-done((bf16[32,7168]{1,0:T(8,128)(2,1)S(1)}, bf16[32,7168]{1,0:T(8,128)(2,1)S(1)}, u32[]{:S(2)}, u32[]{:S(2)}) %collective-permute-start.33) | collective-permute-done | bytes 458784 | tf_op jit(solution)/shard_map/ppermute | solution.py:37
  143.2 12.3 %collective-permute-done.29 = bf16[96,7168]{1,0:T(8,128)(2,1)S(1)} collective-permute-done((bf16[96,7168]{1,0:T(8,128)(2,1)S(1)}, bf16[96,7168]{1,0:T(8,128)(2,1)S(1)}, u32[]{:S(2)}, u32[]{:S(2)}) %collective-permute-start.29) | collective-permute-done | bytes 1376288 | tf_op jit(solution)/shard_map/ppermute | solution.py:37
  155.5 3.4 %collective-permute-done.31 = bf16[96,7168]{1,0:T(8,128)(2,1)S(1)} collective-permute-done((bf16[96,7168]{1,0:T(8,128)(2,1)S(1)}, bf16[96,7168]{1,0:T(8,128)(2,1)S(1)}, u32[]{:S(2)}, u32[]{:S(2)}) %collective-permute-start.31) | collective-permute-done | bytes 1376288 | tf_op jit(solution)/shard_map/ppermute | solution.py:37
  162.1 5.1 %collective-permute-done.35 = bf16[32,7168]{1,0:T(8,128)(2,1)S(1)} collective-permute-done((bf16[32,7168]{1,0:T(8,128)(2,1)S(1)}, bf16[32,7168]{1,0:T(8,128)(2,1)S(1)}, u32[]{:S(2)}, u32[]{:S(2)}) %collective-permute-start.35) | collective-permute-done | bytes 458784 | tf_op jit(solution)/shard_map/ppermute | solution.py:37
  167.2 3.1 %collective-permute-done.37 = bf16[32,7168]{1,0:T(8,128)(2,1)S(1)} collective-permute-done((bf16[32,7168]{1,0:T(8,128)(2,1)S(1)}, bf16[32,7168]{1,0:T(8,128)(2,1)S(1)}, u32[]{:S(2)}, u32[]{:S(2)}) %collective-permute-start.37) | collective-permute-done | bytes 458784 | tf_op jit(solution)/shard_map/ppermute | solution.py:37
  174.6 3.1 %collective-permute-done.39 = bf16[8,7168]{1,0:T(8,128)(2,1)S(1)} collective-permute-done((bf16[8,7168]{1,0:T(8,128)(2,1)S(1)}, bf16[8,7168]{1,0:T(8,128)(2,1)S(1)}, u32[]{:S(2)}, u32[]{:S(2)}) %collective-permute-start.39) | collective-permute-done | bytes 114720 | tf_op jit(solution)/shard_map/ppermute | solution.py:37
  (116 shorter events, 41.0 us)
Async XLA Ops:
  12.1 10.6 %collective-permute-start.3 = (bf16[32,7296]{1,0:T(8,128)(2,1)S(1)}, bf16[32,7296]{1,0:T(8,128)(2,1)S(1)}, u32[]{:S(2)}, u32[]{:S(2)}) collective-permute-start(bf16[32,7296]{1,0:T(8,128)(2,1)S(1)} %pad_maximum_fusion.refs_0_), channel_id=1, source_target_pairs={{0,8},{1,3},{2,10},{3,5},{4,12},{5,7},{6,14},{7,1},{8,16},{9,11},{... | collective-permute-start | bytes 1400840 | tf_op jit(solution)/shard_map/ppermute | solution.py:37
  14.0 8.7 %collective-permute-start.4 = (bf16[32,7296]{1,0:T(8,128)(2,1)S(1)}, bf16[32,7296]{1,0:T(8,128)(2,1)S(1)}, u32[]{:S(2)}, u32[]{:S(2)}) collective-permute-start(bf16[32,7296]{1,0:T(8,128)(2,1)S(1)} %pad_maximum_fusion.refs_0_), channel_id=1, source_target_pairs={{0,24},{1,7},{2,26},{3,1},{4,28},{5,3},{6,30},{7,5},{8,0},{9,15},{... | collective-permute-start | bytes 1400840 | tf_op jit(solution)/shard_map/ppermute | solution.py:37
  23.9 28.2 %collective-permute-start.10 = (bf16[96,7296]{1,0:T(8,128)(2,1)}, bf16[96,7296]{1,0:T(8,128)(2,1)}, u32[]{:S(2)}, u32[]{:S(2)}) collective-permute-start(bf16[96,7296]{1,0:T(8,128)(2,1)} %pack.2.refs_0_), channel_id=1, source_target_pairs={{0,32},{1,9},{2,34},{3,11},{4,36},{5,13},{6,38},{7,15},{8,40},{9,1... | collective-permute-start | bytes 4202504 | tf_op jit(solution)/shard_map/ppermute | solution.py:37
  24.9 33.7 %collective-permute-start.14 = (bf16[96,7296]{1,0:T(8,128)(2,1)}, bf16[96,7296]{1,0:T(8,128)(2,1)S(1)}, u32[]{:S(2)}, u32[]{:S(2)}) collective-permute-start(bf16[96,7296]{1,0:T(8,128)(2,1)} %pack.2.refs_0_), channel_id=1, source_target_pairs={{0,96},{1,25},{2,98},{3,27},{4,100},{5,29},{6,102},{7,31},{8,104},... | collective-permute-start | bytes 4202504 | tf_op jit(solution)/shard_map/ppermute | solution.py:37
  26.6 6.7 %collective-permute-start.5 = (bf16[16,7296]{1,0:T(8,128)(2,1)S(1)}, bf16[16,7296]{1,0:T(8,128)(2,1)S(1)}, u32[]{:S(2)}, u32[]{:S(2)}) collective-permute-start(bf16[16,7296]{1,0:T(8,128)(2,1)S(1)} %slice.60), channel_id=1, source_target_pairs={{0,8},{1,3},{2,10},{3,5},{4,12},{5,7},{6,14},{7,1},{8,16},{9,11},{... | collective-permute-start | bytes 700424 | tf_op jit(solution)/shard_map/ppermute | solution.py:37
  33.3 17.2 %collective-permute-start.12 = (bf16[32,7296]{1,0:T(8,128)(2,1)S(1)}, bf16[32,7296]{1,0:T(8,128)(2,1)S(1)}, u32[]{:S(2)}, u32[]{:S(2)}) collective-permute-start(bf16[32,7296]{1,0:T(8,128)(2,1)S(1)} %pack.3.refs_1_), channel_id=1, source_target_pairs={{0,32},{1,9},{2,34},{3,11},{4,36},{5,13},{6,38},{7,15},{8,40},{9,1... | collective-permute-start | bytes 1400840 | tf_op jit(solution)/shard_map/ppermute | solution.py:37
  33.4 36.5 %collective-permute-start.7 = (bf16[96,7296]{1,0:T(8,128)(2,1)}, bf16[96,7296]{1,0:T(8,128)(2,1)}, u32[]{:S(2)}, u32[]{:S(2)}) collective-permute-start(bf16[96,7296]{1,0:T(8,128)(2,1)} %pack.2.refs_0_), channel_id=1, source_target_pairs={{0,1},{1,0},{2,3},{3,2},{4,5},{5,4},{6,7},{7,6},{8,9},{9,8},{10,11... | collective-permute-start | bytes 4202504 | tf_op jit(solution)/shard_map/ppermute | solution.py:41
  40.8 12.6 %collective-permute-start.8 = (bf16[32,7296]{1,0:T(8,128)(2,1)S(1)}, bf16[32,7296]{1,0:T(8,128)(2,1)S(1)}, u32[]{:S(2)}, u32[]{:S(2)}) collective-permute-start(bf16[32,7296]{1,0:T(8,128)(2,1)S(1)} %pack.3.refs_1_), channel_id=1, source_target_pairs={{0,1},{1,0},{2,3},{3,2},{4,5},{5,4},{6,7},{7,6},{8,9},{9,8},{10,11... | collective-permute-start | bytes 1400840 | tf_op jit(solution)/shard_map/ppermute | solution.py:41
  50.6 7.7 %collective-permute-start.16 = (bf16[32,7296]{1,0:T(8,128)(2,1)S(1)}, bf16[32,7296]{1,0:T(8,128)(2,1)S(1)}, u32[]{:S(2)}, u32[]{:S(2)}) collective-permute-start(bf16[32,7296]{1,0:T(8,128)(2,1)S(1)} %pack.3.refs_1_), channel_id=1, source_target_pairs={{0,96},{1,25},{2,98},{3,27},{4,100},{5,29},{6,102},{7,31},{8,104},... | collective-permute-start | bytes 1400840 | tf_op jit(solution)/shard_map/ppermute | solution.py:37
  52.0 32.4 %collective-permute-start.22 = (bf16[96,7296]{1,0:T(8,128)(2,1)}, bf16[96,7296]{1,0:T(8,128)(2,1)}, u32[]{:S(2)}, u32[]{:S(2)}) collective-permute-start(bf16[96,7296]{1,0:T(8,128)(2,1)} %collective-permute-done.10.refs_0_.refs_4_), channel_id=1, source_target_pairs={{0,1},{1,0},{2,3},{3,2},{4,5},{5,4},{6,7},{7,6},{8,9},{9,8},{10,11... | collective-permute-start | bytes 4202504 | tf_op jit(solution)/shard_map/ppermute | solution.py:41
  54.3 6.5 %collective-permute-start.13 = (bf16[16,7296]{1,0:T(8,128)(2,1)S(1)}, bf16[16,7296]{1,0:T(8,128)(2,1)S(1)}, u32[]{:S(2)}, u32[]{:S(2)}) collective-permute-start(bf16[16,7296]{1,0:T(8,128)(2,1)S(1)} %slice.63), channel_id=1, source_target_pairs={{0,32},{1,9},{2,34},{3,11},{4,36},{5,13},{6,38},{7,15},{8,40},{9,1... | collective-permute-start | bytes 700424 | tf_op jit(solution)/shard_map/ppermute | solution.py:37
  58.3 12.8 %collective-permute-start.11 = (bf16[48,7296]{1,0:T(8,128)(2,1)}, bf16[48,7296]{1,0:T(8,128)(2,1)}, u32[]{:S(2)}, u32[]{:S(2)}) collective-permute-start(bf16[48,7296]{1,0:T(8,128)(2,1)} %slice.62), channel_id=1, source_target_pairs={{0,32},{1,9},{2,34},{3,11},{4,36},{5,13},{6,38},{7,15},{8,40},{9,1... | collective-permute-start | bytes 2101256 | tf_op jit(solution)/shard_map/ppermute | solution.py:37
  58.6 32.6 %collective-permute-start.24 = (bf16[96,7296]{1,0:T(8,128)(2,1)S(1)}, bf16[96,7296]{1,0:T(8,128)(2,1)}, u32[]{:S(2)}, u32[]{:S(2)}) collective-permute-start(bf16[96,7296]{1,0:T(8,128)(2,1)S(1)} %collective-permute-done.14.refs_2_.refs_6_), channel_id=1, source_target_pairs={{0,1},{1,0},{2,3},{3,2},{4,5},{5,4},{6,7},{7,6},{8,9},{9,8},{10,11... | collective-permute-start | bytes 4202504 | tf_op jit(solution)/shard_map/ppermute | solution.py:41
  66.5 17.9 %collective-permute-start.15 = (bf16[48,7296]{1,0:T(8,128)(2,1)}, bf16[48,7296]{1,0:T(8,128)(2,1)}, u32[]{:S(2)}, u32[]{:S(2)}) collective-permute-start(bf16[48,7296]{1,0:T(8,128)(2,1)} %slice.64), channel_id=1, source_target_pairs={{0,96},{1,25},{2,98},{3,27},{4,100},{5,29},{6,102},{7,31},{8,104},... | collective-permute-start | bytes 2101256 | tf_op jit(solution)/shard_map/ppermute | solution.py:37
  70.0 20.6 %collective-permute-start.23 = (bf16[32,7296]{1,0:T(8,128)(2,1)S(1)}, bf16[32,7296]{1,0:T(8,128)(2,1)S(1)}, u32[]{:S(2)}, u32[]{:S(2)}) collective-permute-start(bf16[32,7296]{1,0:T(8,128)(2,1)S(1)} %collective-permute-done.12.refs_1_.refs_5_), channel_id=1, source_target_pairs={{0,1},{1,0},{2,3},{3,2},{4,5},{5,4},{6,7},{7,6},{8,9},{9,8},{10,11... | collective-permute-start | bytes 1400840 | tf_op jit(solution)/shard_map/ppermute | solution.py:41
  71.1 19.8 %collective-permute-start.25 = (bf16[32,7296]{1,0:T(8,128)(2,1)S(1)}, bf16[32,7296]{1,0:T(8,128)(2,1)S(1)}, u32[]{:S(2)}, u32[]{:S(2)}) collective-permute-start(bf16[32,7296]{1,0:T(8,128)(2,1)S(1)} %collective-permute-done.16.refs_3_.refs_7_), channel_id=1, source_target_pairs={{0,1},{1,0},{2,3},{3,2},{4,5},{5,4},{6,7},{7,6},{8,9},{9,8},{10,11... | collective-permute-start | bytes 1400840 | tf_op jit(solution)/shard_map/ppermute | solution.py:41
  84.4 15.5 %collective-permute-start.18 = (bf16[48,7296]{1,0:T(8,128)(2,1)}, bf16[48,7296]{1,0:T(8,128)(2,1)S(1)}, u32[]{:S(2)}, u32[]{:S(2)}) collective-permute-start(bf16[48,7296]{1,0:T(8,128)(2,1)} %collective-permute-done.11.refs_0_.refs_8_), channel_id=1, source_target_pairs={{0,1},{1,0},{2,3},{3,2},{4,5},{5,4},{6,7},{7,6},{8,9},{9,8},{10,11... | collective-permute-start | bytes 2101256 | tf_op jit(solution)/shard_map/ppermute | solution.py:41
  84.5 15.4 %collective-permute-start.20 = (bf16[48,7296]{1,0:T(8,128)(2,1)}, bf16[48,7296]{1,0:T(8,128)(2,1)S(1)}, u32[]{:S(2)}, u32[]{:S(2)}) collective-permute-start(bf16[48,7296]{1,0:T(8,128)(2,1)} %collective-permute-done.15.refs_2_.refs_10_), channel_id=1, source_target_pairs={{0,1},{1,0},{2,3},{3,2},{4,5},{5,4},{6,7},{7,6},{8,9},{9,8},{10,11... | collective-permute-start | bytes 2101256 | tf_op jit(solution)/shard_map/ppermute | solution.py:41
  90.6 9.2 %collective-permute-start.19 = (bf16[16,7296]{1,0:T(8,128)(2,1)S(1)}, bf16[16,7296]{1,0:T(8,128)(2,1)S(1)}, u32[]{:S(2)}, u32[]{:S(2)}) collective-permute-start(bf16[16,7296]{1,0:T(8,128)(2,1)S(1)} %copy-done.4), channel_id=1, source_target_pairs={{0,1},{1,0},{2,3},{3,2},{4,5},{5,4},{6,7},{7,6},{8,9},{9,8},{10,11... | collective-permute-start | bytes 700424 | tf_op jit(solution)/shard_map/ppermute | solution.py:41
  91.0 8.9 %collective-permute-start.21 = (bf16[16,7296]{1,0:T(8,128)(2,1)S(1)}, bf16[16,7296]{1,0:T(8,128)(2,1)S(1)}, u32[]{:S(2)}, u32[]{:S(2)}) collective-permute-start(bf16[16,7296]{1,0:T(8,128)(2,1)S(1)} %copy-done.6), channel_id=1, source_target_pairs={{0,1},{1,0},{2,3},{3,2},{4,5},{5,4},{6,7},{7,6},{8,9},{9,8},{10,11... | collective-permute-start | bytes 700424 | tf_op jit(solution)/shard_map/ppermute | solution.py:41
  99.9 10.4 %collective-permute-start.26 = (bf16[256,7168]{1,0:T(8,128)(2,1)S(1)}, bf16[256,7168]{1,0:T(8,128)(2,1)S(1)}, u32[]{:S(2)}, u32[]{:S(2)}) collective-permute-start(bf16[256,7168]{1,0:T(8,128)(2,1)S(1)} %outputs.8), channel_id=1, source_target_pairs={{0,1},{1,0},{2,3},{3,2},{4,5},{5,4},{6,7},{7,6},{8,9},{9,8},{10,11... | collective-permute-start | bytes 11010056 | tf_op jit(solution)/shard_map/ppermute | solution.py:41
  109.9 23.0 %collective-permute-start.9 = (bf16[128,7168]{1,0:T(8,128)(2,1)S(1)}, bf16[128,7168]{1,0:T(8,128)(2,1)S(1)}, u32[]{:S(2)}, u32[]{:S(2)}) collective-permute-start(bf16[128,7168]{1,0:T(8,128)(2,1)S(1)} %outputs.6), channel_id=1, source_target_pairs={{0,1},{1,0},{2,3},{3,2},{4,5},{5,4},{6,7},{7,6},{8,9},{9,8},{10,11... | collective-permute-start | bytes 5505032 | tf_op jit(solution)/shard_map/ppermute | solution.py:41
  115.5 13.0 %collective-permute-start.28 = (bf16[64,7168]{1,0:T(8,128)(2,1)S(1)}, bf16[64,7168]{1,0:T(8,128)(2,1)S(1)}, u32[]{:S(2)}, u32[]{:S(2)}) collective-permute-start(bf16[64,7168]{1,0:T(8,128)(2,1)S(1)} %get-tuple-element.48), channel_id=1, source_target_pairs={{0,96},{1,25},{2,98},{3,27},{4,100},{5,29},{6,102},{7,31},{8,104},... | collective-permute-start | bytes 2752520 | tf_op jit(solution)/shard_map/ppermute | solution.py:37
  118.1 13.9 %collective-permute-start.30 = (bf16[64,7168]{1,0:T(8,128)(2,1)S(1)}, bf16[64,7168]{1,0:T(8,128)(2,1)S(1)}, u32[]{:S(2)}, u32[]{:S(2)}) collective-permute-start(bf16[64,7168]{1,0:T(8,128)(2,1)S(1)} %get-tuple-element.50), channel_id=1, source_target_pairs={{0,32},{1,9},{2,34},{3,11},{4,36},{5,13},{6,38},{7,15},{8,40},{9,1... | collective-permute-start | bytes 2752520 | tf_op jit(solution)/shard_map/ppermute | solution.py:37
  128.5 9.5 %collective-permute-start.32 = (bf16[32,7168]{1,0:T(8,128)(2,1)S(1)}, bf16[32,7168]{1,0:T(8,128)(2,1)S(1)}, u32[]{:S(2)}, u32[]{:S(2)}) collective-permute-start(bf16[32,7168]{1,0:T(8,128)(2,1)S(1)} %merge.8), channel_id=1, source_target_pairs={{0,96},{1,25},{2,98},{3,27},{4,100},{5,29},{6,102},{7,31},{8,104},... | collective-permute-start | bytes 1376264 | tf_op jit(solution)/shard_map/ppermute | solution.py:37
  132.1 9.1 %collective-permute-start.33 = (bf16[32,7168]{1,0:T(8,128)(2,1)S(1)}, bf16[32,7168]{1,0:T(8,128)(2,1)S(1)}, u32[]{:S(2)}, u32[]{:S(2)}) collective-permute-start(bf16[32,7168]{1,0:T(8,128)(2,1)S(1)} %merge.9), channel_id=1, source_target_pairs={{0,32},{1,9},{2,34},{3,11},{4,36},{5,13},{6,38},{7,15},{8,40},{9,1... | collective-permute-start | bytes 1376264 | tf_op jit(solution)/shard_map/ppermute | solution.py:37
  135.0 20.4 %collective-permute-start.29 = (bf16[96,7168]{1,0:T(8,128)(2,1)S(1)}, bf16[96,7168]{1,0:T(8,128)(2,1)S(1)}, u32[]{:S(2)}, u32[]{:S(2)}) collective-permute-start(bf16[96,7168]{1,0:T(8,128)(2,1)S(1)} %merge.6), channel_id=1, source_target_pairs={{0,96},{1,25},{2,98},{3,27},{4,100},{5,29},{6,102},{7,31},{8,104},... | collective-permute-start | bytes 4128776 | tf_op jit(solution)/shard_map/ppermute | solution.py:37
  138.0 20.9 %collective-permute-start.31 = (bf16[96,7168]{1,0:T(8,128)(2,1)S(1)}, bf16[96,7168]{1,0:T(8,128)(2,1)S(1)}, u32[]{:S(2)}, u32[]{:S(2)}) collective-permute-start(bf16[96,7168]{1,0:T(8,128)(2,1)S(1)} %merge.7), channel_id=1, source_target_pairs={{0,32},{1,9},{2,34},{3,11},{4,36},{5,13},{6,38},{7,15},{8,40},{9,1... | collective-permute-start | bytes 4128776 | tf_op jit(solution)/shard_map/ppermute | solution.py:37
  141.4 18.1 %collective-permute-start.34 = (bf16[16,7168]{1,0:T(8,128)(2,1)S(1)}, bf16[16,7168]{1,0:T(8,128)(2,1)S(1)}, u32[]{:S(2)}, u32[]{:S(2)}) collective-permute-start(bf16[16,7168]{1,0:T(8,128)(2,1)S(1)} %get-tuple-element.59), channel_id=1, source_target_pairs={{0,24},{1,7},{2,26},{3,1},{4,28},{5,3},{6,30},{7,5},{8,0},{9,15},{... | collective-permute-start | bytes 688136 | tf_op jit(solution)/shard_map/ppermute | solution.py:37
  143.2 18.1 %collective-permute-start.36 = (bf16[16,7168]{1,0:T(8,128)(2,1)S(1)}, bf16[16,7168]{1,0:T(8,128)(2,1)S(1)}, u32[]{:S(2)}, u32[]{:S(2)}) collective-permute-start(bf16[16,7168]{1,0:T(8,128)(2,1)S(1)} %get-tuple-element.60), channel_id=1, source_target_pairs={{0,8},{1,3},{2,10},{3,5},{4,12},{5,7},{6,14},{7,1},{8,16},{9,11},{... | collective-permute-start | bytes 688136 | tf_op jit(solution)/shard_map/ppermute | solution.py:37
  159.5 7.7 %collective-permute-start.35 = (bf16[32,7168]{1,0:T(8,128)(2,1)S(1)}, bf16[32,7168]{1,0:T(8,128)(2,1)S(1)}, u32[]{:S(2)}, u32[]{:S(2)}) collective-permute-start(bf16[32,7168]{1,0:T(8,128)(2,1)S(1)} %merge.10), channel_id=1, source_target_pairs={{0,24},{1,7},{2,26},{3,1},{4,28},{5,3},{6,30},{7,5},{8,0},{9,15},{... | collective-permute-start | bytes 1376264 | tf_op jit(solution)/shard_map/ppermute | solution.py:37
  161.4 8.9 %collective-permute-start.37 = (bf16[32,7168]{1,0:T(8,128)(2,1)S(1)}, bf16[32,7168]{1,0:T(8,128)(2,1)S(1)}, u32[]{:S(2)}, u32[]{:S(2)}) collective-permute-start(bf16[32,7168]{1,0:T(8,128)(2,1)S(1)} %merge.11), channel_id=1, source_target_pairs={{0,8},{1,3},{2,10},{3,5},{4,12},{5,7},{6,14},{7,1},{8,16},{9,11},{... | collective-permute-start | bytes 1376264 | tf_op jit(solution)/shard_map/ppermute | solution.py:37
  (23 other events, 260.4 us)

commit v2 on v1

--- a/solution.py
+++ b/solution.py
@@ -99,6 +99,28 @@
         compiler_params=pltpu.CompilerParams(vmem_limit_bytes=vmem_share),
         name="merge",
     )(block, via)
+
+
+def settle(upper, lower, via_a, via_b):
+    half, width = via_a.shape
+    size = 2 * half
+
+    def kernel(*refs):
+        top = sum(widen(r[...]) for r in refs[:3])
+        bottom = sum(widen(r[...]) for r in refs[3:6])
+        first_ref, second_ref, third_ref = refs[8:]
+        first_ref[...] = narrow(top[:size])
+        second_ref[:half] = narrow(top[size:] + widen(refs[6][...]))
+        second_ref[half:] = narrow(bottom[:half])
+        third_ref[:half] = narrow(bottom[half:size])
+        third_ref[half:] = narrow(bottom[size:] + widen(refs[7][...]))
+
+    return pl.pallas_call(
+        kernel,
+        out_shape=[jax.ShapeDtypeStruct((size, width), via_a.dtype)] * 3,
+        compiler_params=pltpu.CompilerParams(vmem_limit_bytes=vmem_share + (8 << 20)),
+        name="settle",
+    )(*upper, *lower, via_a, via_b)
 
 
 def prepare(stream, norm_gain, expert_ids, route_weights):
@@ -370,34 +392,40 @@
     hid_near_2 = hidden_of([behind_a2, behind_b2, ahead_a2, ahead_b2], w_gate, w_up, first_expert)
     far = [far_wide_a, far_slim_a, far_wide_b, far_slim_b]
     far_2 = [swap(f) for f in far]
-    (near_2,) = outputs_of(hid_near_2, 0, [2 * block], down)
-    *far_2, near_2 = after((*far_2, near_2))
-    near_got = swap(near_2)
+    *far_2, hid_near_2 = after((*far_2, hid_near_2))
     hid_far = hidden_of(far + far_2, w_gate, w_up, first_expert)
     (far_part,) = outputs_of(hid_far, 1, [block], down)
-    hid_near, far_part = after((hid_near, far_part))
     far_got = swap(far_part)
-    near = outputs_of(hid_near, 0, [near_rows, size, near_rows, size], down, near_got)
-    hid_far, *near = after((hid_far, *near))
+    hid_near_2, far_part = after((hid_near_2, far_part))
+    (near_2,) = outputs_of(hid_near_2, 0, [2 * block], down)
+    hid_far, near_2 = after((hid_far, near_2))
+    near_got = swap(near_2)
     far_a, far_b = outputs_of(hid_far, 0, [block // 2, block // 2], down, far_got)
 
     via_a = move(far_a, 2, -1)
     via_b = move(far_b, 2, 1)
+    pieces = [near_half, near_half, size]
+    behind_1, behind_2, behind_b, ahead_1, ahead_2, ahead_b = outputs_of(
+        hid_near, 0, pieces + pieces, down, near_got
+    )
+    even_got_a = move(behind_2, 2, -1)
+    even_got_b = move(ahead_1, 2, 1)
     (own_2,) = outputs_of(hid_own, 1, [block], down)
     own_got = swap(own_2)
-    mine_a, mine_b = outputs_of(hid_own, 0, [near_rows, size], down, own_got)
-    behind_a, behind_b, ahead_a, ahead_b = near
+    mine_1, mine_2, mine_b = outputs_of(hid_own, 0, pieces, down, own_got)
     slim_got_a = move(merge(behind_b, via_a, 0, near_half, half), 2, -1)
     slim_got_b = move(merge(ahead_b, via_b, half, near_half, half), 2, 1)
-    wide_got_a = move(merge(behind_a, via_a, 0, 0, near_half), 2, -1)
-    wide_got_b = move(merge(ahead_a, via_b, near_half, 0, near_half), 2, 1)
+    odd_got_a = move(merge(behind_1, via_a, 0, 0, near_half), 2, -1)
+    odd_got_b = move(merge(ahead_2, via_b, 0, 0, near_half), 2, 1)
     slim = narrow(widen(mine_b) + widen(slim_got_a) + widen(slim_got_b))
     line_via_a = move(slim[:half], 1, -1)
     line_via_b = move(slim[half:], 1, 1)
-    wide = narrow(widen(mine_a) + widen(wide_got_a) + widen(wide_got_b))
-    line_got_a = move(merge(wide[size : 2 * size], line_via_a, 0, 0, half), 1, -1)
-    line_got_b = move(merge(wide[2 * size :], line_via_b, half, 0, half), 1, 1)
-    line_sum = narrow(widen(wide[:size]) + widen(line_got_a) + widen(line_got_b))
+    own_line, line_b, line_a = settle(
+        [mine_1, odd_got_a, even_got_b], [mine_2, even_got_a, odd_got_b], line_via_a, line_via_b
+    )
+    line_got_a = move(line_b, 1, -1)
+    line_got_b = move(line_a, 1, 1)
+    line_sum = narrow(widen(own_line) + widen(line_got_a) + widen(line_got_b))
     expert_sum = fold_direct(
         line_sum[:row_count],
         line_sum[row_count : 2 * row_count],

time: 181 us -> 184 us (1.017)
  the two profiles are of different devices: /device:TPU:1 before, /device:TPU:0 now
where the time goes in v2:
time: 184 us; the launch traced here: 183 us
  waiting for transfers between devices  78 us (42%)
  starting transfers between devices  49.5 us (27%)
  Pallas kernels  44.1 us (24%)
  local copies, waits for them, and re-layouts  5.89 us (3%)
  matrix products  2.42 us (1%)
  other arithmetic  2.27 us (1%)
    ppermute x30, waiting for transfers between devices, move(): return lax.ppermute(block, TORUS, torus_pairs(phase, step))  71.5 us
    ppermute x30, starting transfers between devices, move(): return lax.ppermute(block, TORUS, torus_pairs(phase, step))  46.6 us
    pallas_call x3, Pallas kernels, hidden_of(): pl.pallas_call(kernel, grid=(steps,), in_specs=[pl.BlockSpec(memory_space...  17.1 us
    pallas_call x6, Pallas kernels, outputs_of(): pl.pallas_call(kernel, grid=(steps,), in_specs=specs, out_specs=[pl.Block...  13.7 us
    pallas_call x1, Pallas kernels, first_hidden(): pl.pallas_call(kernel, in_specs=[pl.BlockSpec(memory_space=pltpu.SMEM)] +...  9.27 us
    ppermute x13, waiting for transfers between devices, swap(): return lax.ppermute(block, 'ep_2', [(0, 1), (1, 0)])  6.45 us
  transfers between devices with their start and end apart: 43, of which 19 were waited for; matrix products, arithmetic and copies ran while one was open for 3% of the time, Pallas kernels for 16%

profile of v2, /device:TPU:0, one launch (start us, length us, event | category | flops | bytes accessed | tf_op | source)
XLA Modules:
  0.0 183.2 jit_solution(7582199768391385257)
XLA Ops:
  2.5 2.0 %collective-permute-start = (bf16[8,7296]{1,0:T(8,128)(2,1)}, bf16[8,7296]{1,0:T(8,128)(2,1)S(1)}, u32[]{:S(2)}, u32[]{:S(2)}) collective-permute-start(bf16[8,7296]{1,0:T(8,128)(2,1)} %prepare.1), channel_id=1, source_target_pairs={{0,2},{1,33},{2,4},{3,35},{4,6},{5,37},{6,0},{7,39},{8,10},{9,41},... | collective-permute-start | bytes 350216 | tf_op jit(solution)/shard_map/ppermute | solution.py:37
  4.5 2.1 %collective-permute-start.1 = (bf16[8,7296]{1,0:T(8,128)(2,1)}, bf16[8,7296]{1,0:T(8,128)(2,1)S(1)}, u32[]{:S(2)}, u32[]{:S(2)}) collective-permute-start(bf16[8,7296]{1,0:T(8,128)(2,1)} %prepare.1), channel_id=1, source_target_pairs={{0,6},{1,97},{2,0},{3,99},{4,2},{5,101},{6,4},{7,103},{8,14},{9,10... | collective-permute-start | bytes 350216 | tf_op jit(solution)/shard_map/ppermute | solution.py:37
  9.6 3.5 %collective-permute-done.2 = bf16[8,7296]{1,0:T(8,128)(2,1)S(1)} collective-permute-done((bf16[8,7296]{1,0:T(8,128)(2,1)}, bf16[8,7296]{1,0:T(8,128)(2,1)S(1)}, u32[]{:S(2)}, u32[]{:S(2)}) %collective-permute-start.2) | collective-permute-done | bytes 116768 | tf_op jit(solution)/shard_map/ppermute | solution.py:37
  17.4 6.5 %collective-permute-done.3.refs_1_ = bf16[32,7296]{1,0:T(8,128)(2,1)S(1)} collective-permute-done((bf16[32,7296]{1,0:T(8,128)(2,1)S(1)}, bf16[32,7296]{1,0:T(8,128)(2,1)S(1)}, u32[]{:S(2)}, u32[]{:S(2)}) %collective-permute-start.3) | collective-permute-done | bytes 466976 | tf_op jit(solution)/shard_map/ppermute | solution.py:37
  32.2 6.4 %collective-permute-done.5.refs_0_ = bf16[16,7296]{1,0:T(8,128)(2,1)S(1)} collective-permute-done((bf16[16,7296]{1,0:T(8,128)(2,1)S(1)}, bf16[16,7296]{1,0:T(8,128)(2,1)S(1)}, u32[]{:S(2)}, u32[]{:S(2)}) %collective-permute-start.5) | collective-permute-done | bytes 233504 | tf_op jit(solution)/shard_map/ppermute | solution.py:37
  40.0 10.5 %collective-permute-done.12.refs_1_.refs_5_ = bf16[32,7296]{1,0:T(8,128)(2,1)S(1)} collective-permute-done((bf16[32,7296]{1,0:T(8,128)(2,1)S(1)}, bf16[32,7296]{1,0:T(8,128)(2,1)S(1)}, u32[]{:S(2)}, u32[]{:S(2)}) %collective-permute-start.12) | collective-permute-done | bytes 466976 | tf_op jit(solution)/shard_map/ppermute | solution.py:37
  53.4 2.0 %slice.50 = bf16[48,7296]{1,0:T(8,128)(2,1)} slice(bf16[96,7296]{1,0:T(8,128)(2,1)} %collective-permute-done.10.refs_0_.refs_4_), slice={[0:48], [0:7296]} | slice | bytes 1400832 | tf_op jit(solution)/shard_map/slice | solution.py:382
  55.4 3.7 %collective-permute-done.14.refs_3_.refs_7_ = bf16[32,7296]{1,0:T(8,128)(2,1)S(1)} collective-permute-done((bf16[32,7296]{1,0:T(8,128)(2,1)S(1)}, bf16[32,7296]{1,0:T(8,128)(2,1)S(1)}, u32[]{:S(2)}, u32[]{:S(2)}) %collective-permute-start.14) | collective-permute-done | bytes 466976 | tf_op jit(solution)/shard_map/ppermute | solution.py:37
  60.2 2.3 %collective-permute-start.18 = (bf16[16,7296]{1,0:T(8,128)(2,1)S(1)}, bf16[16,7296]{1,0:T(8,128)(2,1)S(1)}, u32[]{:S(2)}, u32[]{:S(2)}) collective-permute-start(bf16[16,7296]{1,0:T(8,128)(2,1)S(1)} %slice.53), channel_id=1, source_target_pairs={{0,96},{1,25},{2,98},{3,27},{4,100},{5,29},{6,102},{7,31},{8,104},... | collective-permute-start | bytes 700424 | tf_op jit(solution)/shard_map/ppermute | solution.py:37
  63.3 2.9 %collective-permute-done.18.refs_3_.refs_11_ = bf16[16,7296]{1,0:T(8,128)(2,1)S(1)} collective-permute-done((bf16[16,7296]{1,0:T(8,128)(2,1)S(1)}, bf16[16,7296]{1,0:T(8,128)(2,1)S(1)}, u32[]{:S(2)}, u32[]{:S(2)}) %collective-permute-start.18) | collective-permute-done | bytes 233504 | tf_op jit(solution)/shard_map/ppermute | solution.py:37
  66.2 3.5 %collective-permute-start.17 = (bf16[48,7296]{1,0:T(8,128)(2,1)}, bf16[48,7296]{1,0:T(8,128)(2,1)}, u32[]{:S(2)}, u32[]{:S(2)}) collective-permute-start(bf16[48,7296]{1,0:T(8,128)(2,1)} %slice.52), channel_id=1, source_target_pairs={{0,96},{1,25},{2,98},{3,27},{4,100},{5,29},{6,102},{7,31},{8,104},... | collective-permute-start | bytes 2101256 | tf_op jit(solution)/shard_map/ppermute | solution.py:37
  73.7 9.3 %first_hidden.1 = (bf16[256,512]{1,0:T(8,128)(2,1)S(1)}, bf16[2,7168,256]{2,1,0:T(8,128)(2,1)S(1)}, bf16[2,7168,256]{2,1,0:T(8,128)(2,1)S(1)}, bf16[2,256,7168]{2,1,0:T(8,128)(2,1)S(1)}) custom-call(s32[1]{0:T(128)} %bitcast.first_ref, bf16[96,7296]{1,0:T(8,128)(2,1)} %pack.2.refs_0_, bf16[32,7296]{1,0:T(8,128)(2,1)S(1)} %copy-done.2, ...), custom_call_target="tpu_custom_call" | custom-call | flops 3758096384 | bytes 22020096 | tf_op jit(solution)/shard_map/first_hidden/pallas_call | solution.py:196
  83.9 5.6 %hidden.3.refs_0_ = bf16[256,512]{1,0:T(8,128)(2,1)S(1)} custom-call(s32[1]{0:T(128)} %bitcast.first_ref, bf16[96,7296]{1,0:T(8,128)(2,1)} %collective-permute-done.10.refs_0_.refs_4_, bf16[32,7296]{1,0:T(8,128)(2,1)S(1)} %collective-permute-done.12.refs_1_.refs_5_, bf16[96,7296]{1,0:T(8,128)(2,1)S(1)} %collective-permute-done.13.refs_2_.refs_6_, ...), custom_call_target="tpu_custom_call" | custom-call | flops 3758096384 | bytes 18350080 | tf_op jit(solution)/shard_map/hidden/pallas_call | solution.py:252
  90.1 5.7 %hidden.4.refs_0_ = bf16[256,512]{1,0:T(8,128)(2,1)S(1)} custom-call(s32[1]{0:T(128)} %bitcast.first_ref, bf16[96,7296]{1,0:T(8,128)(2,1)} %collective-permute-done.11.refs_0_.refs_4_, bf16[32,7296]{1,0:T(8,128)(2,1)S(1)} %collective-permute-done.23.refs_1_.refs_5_, bf16[96,7296]{1,0:T(8,128)(2,1)} %collective-permute-done.24.refs_2_.refs_6_, ...), custom_call_target="tpu_custom_call" | custom-call | flops 3758096384 | bytes 18350080 | tf_op jit(solution)/shard_map/hidden/pallas_call | solution.py:252
  95.9 5.8 %hidden.5.refs_0_ = bf16[256,512]{1,0:T(8,128)(2,1)S(1)} custom-call(s32[1]{0:T(128)} %bitcast.first_ref, bf16[48,7296]{1,0:T(8,128)(2,1)} %collective-permute-done.15.refs_0_.refs_8_, bf16[16,7296]{1,0:T(8,128)(2,1)S(1)} %copy-done.4, bf16[48,7296]{1,0:T(8,128)(2,1)} %collective-permute-done.17.refs_2_.refs_10_, bf16[16,7296]{1,0:T(8,128)(2,1)S(1)} %copy-done.6, ...), custom_call_target="tpu_custom_call" | custom-call | flops 3758096384 | bytes 18350080 | tf_op jit(solution)/shard_map/hidden/pallas_call | solution.py:252
  103.5 2.9 %outputs.9 = bf16[256,7168]{1,0:T(8,128)(2,1)S(1)} custom-call(bf16[256,512]{1,0:T(8,128)(2,1)S(1)} %hidden.4.refs_0_, bf16[2,256,7168]{2,1,0:T(8,128)(2,1)S(1)} %get-tuple-element.31.refs_1_), custom_call_target="tpu_custom_call" | custom-call | flops 1879048192 | bytes 14680064 | tf_op jit(solution)/shard_map/outputs/pallas_call | solution.py:307
  109.1 6.4 %collective-permute-done.27.refs_2_ = bf16[128,7168]{1,0:T(8,128)(2,1)S(1)} collective-permute-done((bf16[128,7168]{1,0:T(8,128)(2,1)S(1)}, bf16[128,7168]{1,0:T(8,128)(2,1)S(1)}, u32[]{:S(2)}, u32[]{:S(2)}) %collective-permute-start.27) | collective-permute-done | bytes 1835040 | tf_op jit(solution)/shard_map/ppermute | solution.py:41
  115.5 2.0 %outputs.11 = (bf16[64,7168]{1,0:T(8,128)(2,1)S(1)}, bf16[64,7168]{1,0:T(8,128)(2,1)S(1)}) custom-call(bf16[256,512]{1,0:T(8,128)(2,1)S(1)} %hidden.5.refs_0_, bf16[2,256,7168]{2,1,0:T(8,128)(2,1)S(1)} %get-tuple-element.31.refs_1_, bf16[128,7168]{1,0:T(8,128)(2,1)S(1)} %collective-permute-done.27.refs_2_), custom_call_target="tpu_custom_call" | custom-call | flops 939524096 | bytes 11010048 | tf_op jit(solution)/shard_map/outputs/pallas_call | solution.py:307
  119.6 3.2 %outputs.10 = (bf16[48,7168]{1,0:T(8,128)(2,1)S(1)}, bf16[48,7168]{1,0:T(8,128)(2,1)S(1)}, bf16[32,7168]{1,0:T(8,128)(2,1)S(1)}, bf16[48,7168]{1,0:T(8,128)(2,1)...) custom-call(bf16[256,512]{1,0:T(8,128)(2,1)S(1)} %hidden.3.refs_0_, ...), custom_call_target="tpu_custom_call" | custom-call | flops 1879048192 | bytes 14680064 | tf_op jit(solution)/shard_map/outputs/pallas_call | solution.py:307
  122.8 8.2 %collective-permute-done.28.via_ref = bf16[64,7168]{1,0:T(8,128)(2,1)S(1)} collective-permute-done((bf16[64,7168]{1,0:T(8,128)(2,1)S(1)}, bf16[64,7168]{1,0:T(8,128)(2,1)S(1)}, u32[]{:S(2)}, u32[]{:S(2)}) %collective-permute-start.28) | collective-permute-done | bytes 917536 | tf_op jit(solution)/shard_map/ppermute | solution.py:37
  131.0 2.8 %collective-permute-start.34 = (bf16[32,7168]{1,0:T(8,128)(2,1)S(1)}, bf16[32,7168]{1,0:T(8,128)(2,1)S(1)}, u32[]{:S(2)}, u32[]{:S(2)}) collective-permute-start(bf16[32,7168]{1,0:T(8,128)(2,1)S(1)} %merge.6), channel_id=1, source_target_pairs={{0,96},{1,25},{2,98},{3,27},{4,100},{5,29},{6,102},{7,31},{8,104},... | collective-permute-start | bytes 1376264 | tf_op jit(solution)/shard_map/ppermute | solution.py:37
  134.0 2.0 %outputs.7 = (bf16[48,7168]{1,0:T(8,128)(2,1)S(1)}, bf16[48,7168]{1,0:T(8,128)(2,1)S(1)}, bf16[32,7168]{1,0:T(8,128)(2,1)S(1)}) custom-call(bf16[256,512]{1,0:T(8,128)(2,1)S(1)} %get-tuple-element.30.refs_0_, bf16[2,256,7168]{2,1,0:T(8,128)(2,1)S(1)} %get-tuple-element.31.refs_1_, bf16[128,7168]{1,0:T(8,128)(2,1)S(1)} %collective-permute-done.9.refs_2_), custom_call_target="tpu_custom_call" | custom-call | flops 939524096 | bytes 11010048 | tf_op jit(solution)/shard_map/outputs/pallas_call | solution.py:307
  136.7 3.3 %collective-permute-start.29 = (bf16[48,7168]{1,0:T(8,128)(2,1)S(1)}, bf16[48,7168]{1,0:T(8,128)(2,1)S(1)}, u32[]{:S(2)}, u32[]{:S(2)}) collective-permute-start(bf16[48,7168]{1,0:T(8,128)(2,1)S(1)} %merge.4), channel_id=1, source_target_pairs={{0,96},{1,25},{2,98},{3,27},{4,100},{5,29},{6,102},{7,31},{8,104},... | collective-permute-start | bytes 2064392 | tf_op jit(solution)/shard_map/ppermute | solution.py:37
  140.0 3.5 %collective-permute-start.31 = (bf16[48,7168]{1,0:T(8,128)(2,1)S(1)}, bf16[48,7168]{1,0:T(8,128)(2,1)S(1)}, u32[]{:S(2)}, u32[]{:S(2)}) collective-permute-start(bf16[48,7168]{1,0:T(8,128)(2,1)S(1)} %get-tuple-element.49), channel_id=1, source_target_pairs={{0,96},{1,25},{2,98},{3,27},{4,100},{5,29},{6,102},{7,31},{8,104},... | collective-permute-start | bytes 2064392 | tf_op jit(solution)/shard_map/ppermute | solution.py:37
  143.9 2.9 %collective-permute-start.36 = (bf16[16,7168]{1,0:T(8,128)(2,1)S(1)}, bf16[16,7168]{1,0:T(8,128)(2,1)S(1)}, u32[]{:S(2)}, u32[]{:S(2)}) collective-permute-start(bf16[16,7168]{1,0:T(8,128)(2,1)S(1)} %get-tuple-element.62), channel_id=1, source_target_pairs={{0,24},{1,7},{2,26},{3,1},{4,28},{5,3},{6,30},{7,5},{8,0},{9,15},{... | collective-permute-start | bytes 688136 | tf_op jit(solution)/shard_map/ppermute | solution.py:37
  146.8 6.0 %collective-permute-done.36.refs_6_ = bf16[16,7168]{1,0:T(8,128)(2,1)S(1)} collective-permute-done((bf16[16,7168]{1,0:T(8,128)(2,1)S(1)}, bf16[16,7168]{1,0:T(8,128)(2,1)S(1)}, u32[]{:S(2)}, u32[]{:S(2)}) %collective-permute-start.36) | collective-permute-done | bytes 229408 | tf_op jit(solution)/shard_map/ppermute | solution.py:37
  154.5 6.1 %collective-permute-done.37.refs_7_ = bf16[16,7168]{1,0:T(8,128)(2,1)S(1)} collective-permute-done((bf16[16,7168]{1,0:T(8,128)(2,1)S(1)}, bf16[16,7168]{1,0:T(8,128)(2,1)S(1)}, u32[]{:S(2)}, u32[]{:S(2)}) %collective-permute-start.37) | collective-permute-done | bytes 229408 | tf_op jit(solution)/shard_map/ppermute | solution.py:37
  161.1 2.1 %collective-permute-start.38 = (bf16[32,7168]{1,0:T(8,128)(2,1)S(1)}, bf16[32,7168]{1,0:T(8,128)(2,1)S(1)}, u32[]{:S(2)}, u32[]{:S(2)}) collective-permute-start(bf16[32,7168]{1,0:T(8,128)(2,1)S(1)} %get-tuple-element.56), channel_id=1, source_target_pairs={{0,24},{1,7},{2,26},{3,1},{4,28},{5,3},{6,30},{7,5},{8,0},{9,15},{... | collective-permute-start | bytes 1376264 | tf_op jit(solution)/shard_map/ppermute | solution.py:37
  163.9 5.8 %collective-permute-done.38 = bf16[32,7168]{1,0:T(8,128)(2,1)S(1)} collective-permute-done((bf16[32,7168]{1,0:T(8,128)(2,1)S(1)}, bf16[32,7168]{1,0:T(8,128)(2,1)S(1)}, u32[]{:S(2)}, u32[]{:S(2)}) %collective-permute-start.38) | collective-permute-done | bytes 458784 | tf_op jit(solution)/shard_map/ppermute | solution.py:37
  169.7 3.2 %collective-permute-done.39 = bf16[32,7168]{1,0:T(8,128)(2,1)S(1)} collective-permute-done((bf16[32,7168]{1,0:T(8,128)(2,1)S(1)}, bf16[32,7168]{1,0:T(8,128)(2,1)S(1)}, u32[]{:S(2)}, u32[]{:S(2)}) %collective-permute-start.39) | collective-permute-done | bytes 458784 | tf_op jit(solution)/shard_map/ppermute | solution.py:37
  173.1 2.1 %collective-permute-start.40 = (bf16[8,7168]{1,0:T(8,128)(2,1)S(1)}, bf16[8,7168]{1,0:T(8,128)(2,1)S(1)}, u32[]{:S(2)}, u32[]{:S(2)}) collective-permute-start(bf16[8,7168]{1,0:T(8,128)(2,1)S(1)} %get-tuple-element.58), channel_id=1, source_target_pairs={{0,6},{1,97},{2,0},{3,99},{4,2},{5,101},{6,4},{7,103},{8,14},{9,10... | collective-permute-start | bytes 344072 | tf_op jit(solution)/shard_map/ppermute | solution.py:37
  178.7 3.7 %collective-permute-done.41 = bf16[8,7168]{1,0:T(8,128)(2,1)S(1)} collective-permute-done((bf16[8,7168]{1,0:T(8,128)(2,1)S(1)}, bf16[8,7168]{1,0:T(8,128)(2,1)S(1)}, u32[]{:S(2)}, u32[]{:S(2)}) %collective-permute-start.41) | collective-permute-done | bytes 114720 | tf_op jit(solution)/shard_map/ppermute | solution.py:37
  (117 shorter events, 44.0 us)
Async XLA Ops:
  14.1 9.8 %collective-permute-start.3 = (bf16[32,7296]{1,0:T(8,128)(2,1)S(1)}, bf16[32,7296]{1,0:T(8,128)(2,1)S(1)}, u32[]{:S(2)}, u32[]{:S(2)}) collective-permute-start(bf16[32,7296]{1,0:T(8,128)(2,1)S(1)} %pad_maximum_fusion.refs_0_), channel_id=1, source_target_pairs={{0,8},{1,3},{2,10},{3,5},{4,12},{5,7},{6,14},{7,1},{8,16},{9,11},{... | collective-permute-start | bytes 1400840 | tf_op jit(solution)/shard_map/ppermute | solution.py:37
  15.7 8.6 %collective-permute-start.4 = (bf16[32,7296]{1,0:T(8,128)(2,1)S(1)}, bf16[32,7296]{1,0:T(8,128)(2,1)S(1)}, u32[]{:S(2)}, u32[]{:S(2)}) collective-permute-start(bf16[32,7296]{1,0:T(8,128)(2,1)S(1)} %pad_maximum_fusion.refs_0_), channel_id=1, source_target_pairs={{0,24},{1,7},{2,26},{3,1},{4,28},{5,3},{6,30},{7,5},{8,0},{9,15},{... | collective-permute-start | bytes 1400840 | tf_op jit(solution)/shard_map/ppermute | solution.py:37
  25.5 26.5 %collective-permute-start.10 = (bf16[96,7296]{1,0:T(8,128)(2,1)}, bf16[96,7296]{1,0:T(8,128)(2,1)}, u32[]{:S(2)}, u32[]{:S(2)}) collective-permute-start(bf16[96,7296]{1,0:T(8,128)(2,1)} %pack.2.refs_0_), channel_id=1, source_target_pairs={{0,32},{1,9},{2,34},{3,11},{4,36},{5,13},{6,38},{7,15},{8,40},{9,1... | collective-permute-start | bytes 4202504 | tf_op jit(solution)/shard_map/ppermute | solution.py:37
  27.0 32.4 %collective-permute-start.13 = (bf16[96,7296]{1,0:T(8,128)(2,1)}, bf16[96,7296]{1,0:T(8,128)(2,1)S(1)}, u32[]{:S(2)}, u32[]{:S(2)}) collective-permute-start(bf16[96,7296]{1,0:T(8,128)(2,1)} %pack.2.refs_0_), channel_id=1, source_target_pairs={{0,96},{1,25},{2,98},{3,27},{4,100},{5,29},{6,102},{7,31},{8,104},... | collective-permute-start | bytes 4202504 | tf_op jit(solution)/shard_map/ppermute | solution.py:37
  28.8 9.8 %collective-permute-start.5 = (bf16[16,7296]{1,0:T(8,128)(2,1)S(1)}, bf16[16,7296]{1,0:T(8,128)(2,1)S(1)}, u32[]{:S(2)}, u32[]{:S(2)}) collective-permute-start(bf16[16,7296]{1,0:T(8,128)(2,1)S(1)} %slice.48), channel_id=1, source_target_pairs={{0,8},{1,3},{2,10},{3,5},{4,12},{5,7},{6,14},{7,1},{8,16},{9,11},{... | collective-permute-start | bytes 700424 | tf_op jit(solution)/shard_map/ppermute | solution.py:37
  30.4 8.6 %collective-permute-start.6 = (bf16[16,7296]{1,0:T(8,128)(2,1)S(1)}, bf16[16,7296]{1,0:T(8,128)(2,1)S(1)}, u32[]{:S(2)}, u32[]{:S(2)}) collective-permute-start(bf16[16,7296]{1,0:T(8,128)(2,1)S(1)} %slice.49), channel_id=1, source_target_pairs={{0,24},{1,7},{2,26},{3,1},{4,28},{5,3},{6,30},{7,5},{8,0},{9,15},{... | collective-permute-start | bytes 700424 | tf_op jit(solution)/shard_map/ppermute | solution.py:37
  39.1 11.4 %collective-permute-start.12 = (bf16[32,7296]{1,0:T(8,128)(2,1)S(1)}, bf16[32,7296]{1,0:T(8,128)(2,1)S(1)}, u32[]{:S(2)}, u32[]{:S(2)}) collective-permute-start(bf16[32,7296]{1,0:T(8,128)(2,1)S(1)} %pack.3.refs_1_), channel_id=1, source_target_pairs={{0,32},{1,9},{2,34},{3,11},{4,36},{5,13},{6,38},{7,15},{8,40},{9,1... | collective-permute-start | bytes 1400840 | tf_op jit(solution)/shard_map/ppermute | solution.py:37
  39.5 30.3 %collective-permute-start.7 = (bf16[96,7296]{1,0:T(8,128)(2,1)}, bf16[96,7296]{1,0:T(8,128)(2,1)}, u32[]{:S(2)}, u32[]{:S(2)}) collective-permute-start(bf16[96,7296]{1,0:T(8,128)(2,1)} %pack.2.refs_0_), channel_id=1, source_target_pairs={{0,1},{1,0},{2,3},{3,2},{4,5},{5,4},{6,7},{7,6},{8,9},{9,8},{10,11... | collective-permute-start | bytes 4202504 | tf_op jit(solution)/shard_map/ppermute | solution.py:41
  39.5 12.6 %collective-permute-start.8 = (bf16[32,7296]{1,0:T(8,128)(2,1)S(1)}, bf16[32,7296]{1,0:T(8,128)(2,1)S(1)}, u32[]{:S(2)}, u32[]{:S(2)}) collective-permute-start(bf16[32,7296]{1,0:T(8,128)(2,1)S(1)} %pack.3.refs_1_), channel_id=1, source_target_pairs={{0,1},{1,0},{2,3},{3,2},{4,5},{5,4},{6,7},{7,6},{8,9},{9,8},{10,11... | collective-permute-start | bytes 1400840 | tf_op jit(solution)/shard_map/ppermute | solution.py:41
  50.5 8.6 %collective-permute-start.14 = (bf16[32,7296]{1,0:T(8,128)(2,1)S(1)}, bf16[32,7296]{1,0:T(8,128)(2,1)S(1)}, u32[]{:S(2)}, u32[]{:S(2)}) collective-permute-start(bf16[32,7296]{1,0:T(8,128)(2,1)S(1)} %pack.3.refs_1_), channel_id=1, source_target_pairs={{0,96},{1,25},{2,98},{3,27},{4,100},{5,29},{6,102},{7,31},{8,104},... | collective-permute-start | bytes 1400840 | tf_op jit(solution)/shard_map/ppermute | solution.py:37
  52.1 31.5 %collective-permute-start.11 = (bf16[96,7296]{1,0:T(8,128)(2,1)}, bf16[96,7296]{1,0:T(8,128)(2,1)}, u32[]{:S(2)}, u32[]{:S(2)}) collective-permute-start(bf16[96,7296]{1,0:T(8,128)(2,1)} %collective-permute-done.10.refs_0_.refs_4_), channel_id=1, source_target_pairs={{0,1},{1,0},{2,3},{3,2},{4,5},{5,4},{6,7},{7,6},{8,9},{9,8},{10,11... | collective-permute-start | bytes 4202504 | tf_op jit(solution)/shard_map/ppermute | solution.py:41
  59.1 12.6 %collective-permute-start.15 = (bf16[48,7296]{1,0:T(8,128)(2,1)}, bf16[48,7296]{1,0:T(8,128)(2,1)}, u32[]{:S(2)}, u32[]{:S(2)}) collective-permute-start(bf16[48,7296]{1,0:T(8,128)(2,1)} %slice.50), channel_id=1, source_target_pairs={{0,32},{1,9},{2,34},{3,11},{4,36},{5,13},{6,38},{7,15},{8,40},{9,1... | collective-permute-start | bytes 2101256 | tf_op jit(solution)/shard_map/ppermute | solution.py:37
  59.4 30.7 %collective-permute-start.24 = (bf16[96,7296]{1,0:T(8,128)(2,1)S(1)}, bf16[96,7296]{1,0:T(8,128)(2,1)}, u32[]{:S(2)}, u32[]{:S(2)}) collective-permute-start(bf16[96,7296]{1,0:T(8,128)(2,1)S(1)} %collective-permute-done.13.refs_2_.refs_6_), channel_id=1, source_target_pairs={{0,1},{1,0},{2,3},{3,2},{4,5},{5,4},{6,7},{7,6},{8,9},{9,8},{10,11... | collective-permute-start | bytes 4202504 | tf_op jit(solution)/shard_map/ppermute | solution.py:41
  66.2 16.8 %collective-permute-start.17 = (bf16[48,7296]{1,0:T(8,128)(2,1)}, bf16[48,7296]{1,0:T(8,128)(2,1)}, u32[]{:S(2)}, u32[]{:S(2)}) collective-permute-start(bf16[48,7296]{1,0:T(8,128)(2,1)} %slice.52), channel_id=1, source_target_pairs={{0,96},{1,25},{2,98},{3,27},{4,100},{5,29},{6,102},{7,31},{8,104},... | collective-permute-start | bytes 2101256 | tf_op jit(solution)/shard_map/ppermute | solution.py:37
  69.7 19.8 %collective-permute-start.23 = (bf16[32,7296]{1,0:T(8,128)(2,1)S(1)}, bf16[32,7296]{1,0:T(8,128)(2,1)S(1)}, u32[]{:S(2)}, u32[]{:S(2)}) collective-permute-start(bf16[32,7296]{1,0:T(8,128)(2,1)S(1)} %collective-permute-done.12.refs_1_.refs_5_), channel_id=1, source_target_pairs={{0,1},{1,0},{2,3},{3,2},{4,5},{5,4},{6,7},{7,6},{8,9},{9,8},{10,11... | collective-permute-start | bytes 1400840 | tf_op jit(solution)/shard_map/ppermute | solution.py:41
  71.7 18.1 %collective-permute-start.25 = (bf16[32,7296]{1,0:T(8,128)(2,1)S(1)}, bf16[32,7296]{1,0:T(8,128)(2,1)S(1)}, u32[]{:S(2)}, u32[]{:S(2)}) collective-permute-start(bf16[32,7296]{1,0:T(8,128)(2,1)S(1)} %collective-permute-done.14.refs_3_.refs_7_), channel_id=1, source_target_pairs={{0,1},{1,0},{2,3},{3,2},{4,5},{5,4},{6,7},{7,6},{8,9},{9,8},{10,11... | collective-permute-start | bytes 1400840 | tf_op jit(solution)/shard_map/ppermute | solution.py:41
  83.0 12.9 %collective-permute-start.19 = (bf16[48,7296]{1,0:T(8,128)(2,1)}, bf16[48,7296]{1,0:T(8,128)(2,1)S(1)}, u32[]{:S(2)}, u32[]{:S(2)}) collective-permute-start(bf16[48,7296]{1,0:T(8,128)(2,1)} %collective-permute-done.15.refs_0_.refs_8_), channel_id=1, source_target_pairs={{0,1},{1,0},{2,3},{3,2},{4,5},{5,4},{6,7},{7,6},{8,9},{9,8},{10,11... | collective-permute-start | bytes 2101256 | tf_op jit(solution)/shard_map/ppermute | solution.py:41
  83.6 12.3 %collective-permute-start.21 = (bf16[48,7296]{1,0:T(8,128)(2,1)}, bf16[48,7296]{1,0:T(8,128)(2,1)S(1)}, u32[]{:S(2)}, u32[]{:S(2)}) collective-permute-start(bf16[48,7296]{1,0:T(8,128)(2,1)} %collective-permute-done.17.refs_2_.refs_10_), channel_id=1, source_target_pairs={{0,1},{1,0},{2,3},{3,2},{4,5},{5,4},{6,7},{7,6},{8,9},{9,8},{10,11... | collective-permute-start | bytes 2101256 | tf_op jit(solution)/shard_map/ppermute | solution.py:41
  106.4 13.2 %collective-permute-start.26 = (bf16[256,7168]{1,0:T(8,128)(2,1)S(1)}, bf16[256,7168]{1,0:T(8,128)(2,1)S(1)}, u32[]{:S(2)}, u32[]{:S(2)}) collective-permute-start(bf16[256,7168]{1,0:T(8,128)(2,1)S(1)} %outputs.9), channel_id=1, source_target_pairs={{0,1},{1,0},{2,3},{3,2},{4,5},{5,4},{6,7},{7,6},{8,9},{9,8},{10,11... | collective-permute-start | bytes 11010056 | tf_op jit(solution)/shard_map/ppermute | solution.py:41
  106.7 8.8 %collective-permute-start.27 = (bf16[128,7168]{1,0:T(8,128)(2,1)S(1)}, bf16[128,7168]{1,0:T(8,128)(2,1)S(1)}, u32[]{:S(2)}, u32[]{:S(2)}) collective-permute-start(bf16[128,7168]{1,0:T(8,128)(2,1)S(1)} %outputs.8), channel_id=1, source_target_pairs={{0,1},{1,0},{2,3},{3,2},{4,5},{5,4},{6,7},{7,6},{8,9},{9,8},{10,11... | collective-permute-start | bytes 5505032 | tf_op jit(solution)/shard_map/ppermute | solution.py:41
  108.8 25.2 %collective-permute-start.9 = (bf16[128,7168]{1,0:T(8,128)(2,1)S(1)}, bf16[128,7168]{1,0:T(8,128)(2,1)S(1)}, u32[]{:S(2)}, u32[]{:S(2)}) collective-permute-start(bf16[128,7168]{1,0:T(8,128)(2,1)S(1)} %outputs.6), channel_id=1, source_target_pairs={{0,1},{1,0},{2,3},{3,2},{4,5},{5,4},{6,7},{7,6},{8,9},{9,8},{10,11... | collective-permute-start | bytes 5505032 | tf_op jit(solution)/shard_map/ppermute | solution.py:41
  117.5 13.5 %collective-permute-start.28 = (bf16[64,7168]{1,0:T(8,128)(2,1)S(1)}, bf16[64,7168]{1,0:T(8,128)(2,1)S(1)}, u32[]{:S(2)}, u32[]{:S(2)}) collective-permute-start(bf16[64,7168]{1,0:T(8,128)(2,1)S(1)} %get-tuple-element.46), channel_id=1, source_target_pairs={{0,96},{1,25},{2,98},{3,27},{4,100},{5,29},{6,102},{7,31},{8,104},... | collective-permute-start | bytes 2752520 | tf_op jit(solution)/shard_map/ppermute | solution.py:37
  119.1 14.7 %collective-permute-start.32 = (bf16[64,7168]{1,0:T(8,128)(2,1)S(1)}, bf16[64,7168]{1,0:T(8,128)(2,1)S(1)}, u32[]{:S(2)}, u32[]{:S(2)}) collective-permute-start(bf16[64,7168]{1,0:T(8,128)(2,1)S(1)} %get-tuple-element.51), channel_id=1, source_target_pairs={{0,32},{1,9},{2,34},{3,11},{4,36},{5,13},{6,38},{7,15},{8,40},{9,1... | collective-permute-start | bytes 2752520 | tf_op jit(solution)/shard_map/ppermute | solution.py:37
  131.0 9.0 %collective-permute-start.34 = (bf16[32,7168]{1,0:T(8,128)(2,1)S(1)}, bf16[32,7168]{1,0:T(8,128)(2,1)S(1)}, u32[]{:S(2)}, u32[]{:S(2)}) collective-permute-start(bf16[32,7168]{1,0:T(8,128)(2,1)S(1)} %merge.6), channel_id=1, source_target_pairs={{0,96},{1,25},{2,98},{3,27},{4,100},{5,29},{6,102},{7,31},{8,104},... | collective-permute-start | bytes 1376264 | tf_op jit(solution)/shard_map/ppermute | solution.py:37
  133.9 9.8 %collective-permute-start.35 = (bf16[32,7168]{1,0:T(8,128)(2,1)S(1)}, bf16[32,7168]{1,0:T(8,128)(2,1)S(1)}, u32[]{:S(2)}, u32[]{:S(2)}) collective-permute-start(bf16[32,7168]{1,0:T(8,128)(2,1)S(1)} %merge.7), channel_id=1, source_target_pairs={{0,32},{1,9},{2,34},{3,11},{4,36},{5,13},{6,38},{7,15},{8,40},{9,1... | collective-permute-start | bytes 1376264 | tf_op jit(solution)/shard_map/ppermute | solution.py:37
  136.2 24.3 %collective-permute-start.33 = (bf16[48,7168]{1,0:T(8,128)(2,1)S(1)}, bf16[48,7168]{1,0:T(8,128)(2,1)S(1)}, u32[]{:S(2)}, u32[]{:S(2)}) collective-permute-start(bf16[48,7168]{1,0:T(8,128)(2,1)S(1)} %merge.5), channel_id=1, source_target_pairs={{0,32},{1,9},{2,34},{3,11},{4,36},{5,13},{6,38},{7,15},{8,40},{9,1... | collective-permute-start | bytes 2064392 | tf_op jit(solution)/shard_map/ppermute | solution.py:37
  136.7 23.8 %collective-permute-start.29 = (bf16[48,7168]{1,0:T(8,128)(2,1)S(1)}, bf16[48,7168]{1,0:T(8,128)(2,1)S(1)}, u32[]{:S(2)}, u32[]{:S(2)}) collective-permute-start(bf16[48,7168]{1,0:T(8,128)(2,1)S(1)} %merge.4), channel_id=1, source_target_pairs={{0,96},{1,25},{2,98},{3,27},{4,100},{5,29},{6,102},{7,31},{8,104},... | collective-permute-start | bytes 2064392 | tf_op jit(solution)/shard_map/ppermute | solution.py:37
  140.0 20.5 %collective-permute-start.30 = (bf16[48,7168]{1,0:T(8,128)(2,1)S(1)}, bf16[48,7168]{1,0:T(8,128)(2,1)S(1)}, u32[]{:S(2)}, u32[]{:S(2)}) collective-permute-start(bf16[48,7168]{1,0:T(8,128)(2,1)S(1)} %get-tuple-element.47), channel_id=1, source_target_pairs={{0,32},{1,9},{2,34},{3,11},{4,36},{5,13},{6,38},{7,15},{8,40},{9,1... | collective-permute-start | bytes 2064392 | tf_op jit(solution)/shard_map/ppermute | solution.py:37
  140.0 20.5 %collective-permute-start.31 = (bf16[48,7168]{1,0:T(8,128)(2,1)S(1)}, bf16[48,7168]{1,0:T(8,128)(2,1)S(1)}, u32[]{:S(2)}, u32[]{:S(2)}) collective-permute-start(bf16[48,7168]{1,0:T(8,128)(2,1)S(1)} %get-tuple-element.49), channel_id=1, source_target_pairs={{0,96},{1,25},{2,98},{3,27},{4,100},{5,29},{6,102},{7,31},{8,104},... | collective-permute-start | bytes 2064392 | tf_op jit(solution)/shard_map/ppermute | solution.py:37
  143.9 8.9 %collective-permute-start.36 = (bf16[16,7168]{1,0:T(8,128)(2,1)S(1)}, bf16[16,7168]{1,0:T(8,128)(2,1)S(1)}, u32[]{:S(2)}, u32[]{:S(2)}) collective-permute-start(bf16[16,7168]{1,0:T(8,128)(2,1)S(1)} %get-tuple-element.62), channel_id=1, source_target_pairs={{0,24},{1,7},{2,26},{3,1},{4,28},{5,3},{6,30},{7,5},{8,0},{9,15},{... | collective-permute-start | bytes 688136 | tf_op jit(solution)/shard_map/ppermute | solution.py:37
  161.1 8.5 %collective-permute-start.38 = (bf16[32,7168]{1,0:T(8,128)(2,1)S(1)}, bf16[32,7168]{1,0:T(8,128)(2,1)S(1)}, u32[]{:S(2)}, u32[]{:S(2)}) collective-permute-start(bf16[32,7168]{1,0:T(8,128)(2,1)S(1)} %get-tuple-element.56), channel_id=1, source_target_pairs={{0,24},{1,7},{2,26},{3,1},{4,28},{5,3},{6,30},{7,5},{8,0},{9,15},{... | collective-permute-start | bytes 1376264 | tf_op jit(solution)/shard_map/ppermute | solution.py:37
  163.2 9.7 %collective-permute-start.39 = (bf16[32,7168]{1,0:T(8,128)(2,1)S(1)}, bf16[32,7168]{1,0:T(8,128)(2,1)S(1)}, u32[]{:S(2)}, u32[]{:S(2)}) collective-permute-start(bf16[32,7168]{1,0:T(8,128)(2,1)S(1)} %get-tuple-element.57), channel_id=1, source_target_pairs={{0,8},{1,3},{2,10},{3,5},{4,12},{5,7},{6,14},{7,1},{8,16},{9,11},{... | collective-permute-start | bytes 1376264 | tf_op jit(solution)/shard_map/ppermute | solution.py:37
  (25 other events, 308.7 us)

commit v3 on v2

--- a/solution.py
+++ b/solution.py
@@ -14,7 +14,7 @@
 score_scale = 192.0 ** (-0.5)
 norm_eps = 1e-06
 meta_lanes = 128
-vmem_share = 8 << 20
+vmem_share = 12 << 20
 
 PHASE_AXES = ((2, 1, 0), (0, 2, 1))
 
@@ -222,7 +222,7 @@
 
 def hidden_of(blocks, w_gate, w_up, first_expert):
     local_count, width, units = w_gate.shape
-    steps = 2
+    steps = 1
     tile = width // steps
     sizes = [b.shape[0] for b in blocks]
     total = sum(sizes)
@@ -272,7 +272,7 @@
 def outputs_of(hidden, block, sizes, down, got=None):
     width = down.shape[2]
     inner = hidden.shape[1]
-    steps = 4
+    steps = 2
     tile = width // steps
     total = sum(sizes)
 
@@ -357,7 +357,7 @@
     stream_f = widen(stream)
     payload = prepare(stream, norm_gain, expert_ids, route_weights)
 
-    line = jnp.concatenate(spread_direct(payload, 0))
+    line = pack(spread_direct(payload, 0))
     size = line.shape[0]
     half = size // 2
     near_rows = 3 * size

time: 184 us -> 182 us (0.989)
  Pallas kernels: 44.1 us -> 41.2 us
    pallas_call x6, Pallas kernels: 13.7 us -> 11.4 us  [outputs_of(): pl.pallas_call(kernel, grid=(steps,), in_specs=specs, out_specs=[pl.Block...]
    unnamed x28 -> x30, local copies, waits for them, and re-layouts: 2.89 us -> 3.8 us
  transfers between devices with their start and end apart: 43 -> 43, of which waited for: 19 -> 20; matrix products, arithmetic and copies ran while one was open for 3% -> 3% of each run, Pallas kernels for 16% -> 16%
where the time goes in v3:
time: 182 us; the launch traced here: 181 us
  waiting for transfers between devices  79.1 us (43%)
  starting transfers between devices  49.5 us (27%)
  Pallas kernels  41.2 us (23%)
  local copies, waits for them, and re-layouts  6.82 us (4%)
  matrix products  2.42 us (1%)
    ppermute x30, waiting for transfers between devices, move(): return lax.ppermute(block, TORUS, torus_pairs(phase, step))  72.4 us
    ppermute x30, starting transfers between devices, move(): return lax.ppermute(block, TORUS, torus_pairs(phase, step))  46.5 us
    pallas_call x3, Pallas kernels, hidden_of(): pl.pallas_call(kernel, grid=(steps,), in_specs=[pl.BlockSpec(memory_space...  16.4 us
    pallas_call x6, Pallas kernels, outputs_of(): pl.pallas_call(kernel, grid=(steps,), in_specs=specs, out_specs=[pl.Block...  11.4 us
    pallas_call x1, Pallas kernels, first_hidden(): pl.pallas_call(kernel, in_specs=[pl.BlockSpec(memory_space=pltpu.SMEM)] +...  9.27 us
    ppermute x13, waiting for transfers between devices, swap(): return lax.ppermute(block, 'ep_2', [(0, 1), (1, 0)])  6.74 us
    unnamed x30, local copies, waits for them, and re-layouts  3.8 us
  transfers between devices with their start and end apart: 43, of which 20 were waited for; matrix products, arithmetic and copies ran while one was open for 3% of the time, Pallas kernels for 16%

profile of v3, /device:TPU:0, one launch (start us, length us, event | category | flops | bytes accessed | tf_op | source)
XLA Modules:
  0.0 181.3 jit_solution(17988289176287920210)
XLA Ops:
  2.5 2.0 %collective-permute-start = (bf16[8,7296]{1,0:T(8,128)(2,1)}, bf16[8,7296]{1,0:T(8,128)(2,1)S(1)}, u32[]{:S(2)}, u32[]{:S(2)}) collective-permute-start(bf16[8,7296]{1,0:T(8,128)(2,1)} %prepare.1.refs_0_), channel_id=1, source_target_pairs={{0,2},{1,33},{2,4},{3,35},{4,6},{5,37},{6,0},{7,39},{8,10},{9,41},... | collective-permute-start | bytes 350216 | tf_op jit(solution)/shard_map/ppermute | solution.py:37
  4.5 2.1 %collective-permute-start.1 = (bf16[8,7296]{1,0:T(8,128)(2,1)}, bf16[8,7296]{1,0:T(8,128)(2,1)S(1)}, u32[]{:S(2)}, u32[]{:S(2)}) collective-permute-start(bf16[8,7296]{1,0:T(8,128)(2,1)} %prepare.1.refs_0_), channel_id=1, source_target_pairs={{0,6},{1,97},{2,0},{3,99},{4,2},{5,101},{6,4},{7,103},{8,14},{9,10... | collective-permute-start | bytes 350216 | tf_op jit(solution)/shard_map/ppermute | solution.py:37
  9.6 3.5 %collective-permute-done.2.refs_3_ = bf16[8,7296]{1,0:T(8,128)(2,1)S(1)} collective-permute-done((bf16[8,7296]{1,0:T(8,128)(2,1)}, bf16[8,7296]{1,0:T(8,128)(2,1)S(1)}, u32[]{:S(2)}, u32[]{:S(2)}) %collective-permute-start.2) | collective-permute-done | bytes 116768 | tf_op jit(solution)/shard_map/ppermute | solution.py:37
  17.4 6.5 %collective-permute-done.3.refs_1_ = bf16[32,7296]{1,0:T(8,128)(2,1)S(1)} collective-permute-done((bf16[32,7296]{1,0:T(8,128)(2,1)S(1)}, bf16[32,7296]{1,0:T(8,128)(2,1)S(1)}, u32[]{:S(2)}, u32[]{:S(2)}) %collective-permute-start.3) | collective-permute-done | bytes 466976 | tf_op jit(solution)/shard_map/ppermute | solution.py:37
  32.2 6.4 %collective-permute-done.5.refs_0_ = bf16[16,7296]{1,0:T(8,128)(2,1)S(1)} collective-permute-done((bf16[16,7296]{1,0:T(8,128)(2,1)S(1)}, bf16[16,7296]{1,0:T(8,128)(2,1)S(1)}, u32[]{:S(2)}, u32[]{:S(2)}) %collective-permute-start.5) | collective-permute-done | bytes 233504 | tf_op jit(solution)/shard_map/ppermute | solution.py:37
  40.0 10.5 %collective-permute-done.12.refs_1_.refs_5_ = bf16[32,7296]{1,0:T(8,128)(2,1)S(1)} collective-permute-done((bf16[32,7296]{1,0:T(8,128)(2,1)S(1)}, bf16[32,7296]{1,0:T(8,128)(2,1)S(1)}, u32[]{:S(2)}, u32[]{:S(2)}) %collective-permute-start.12) | collective-permute-done | bytes 466976 | tf_op jit(solution)/shard_map/ppermute | solution.py:37
  53.4 2.0 %slice.50 = bf16[48,7296]{1,0:T(8,128)(2,1)} slice(bf16[96,7296]{1,0:T(8,128)(2,1)} %collective-permute-done.10.refs_0_.refs_4_), slice={[0:48], [0:7296]} | slice | bytes 1400832 | tf_op jit(solution)/shard_map/slice | solution.py:382
  55.4 3.7 %collective-permute-done.14.refs_3_.refs_7_ = bf16[32,7296]{1,0:T(8,128)(2,1)S(1)} collective-permute-done((bf16[32,7296]{1,0:T(8,128)(2,1)S(1)}, bf16[32,7296]{1,0:T(8,128)(2,1)S(1)}, u32[]{:S(2)}, u32[]{:S(2)}) %collective-permute-start.14) | collective-permute-done | bytes 466976 | tf_op jit(solution)/shard_map/ppermute | solution.py:37
  60.2 2.2 %collective-permute-start.18 = (bf16[16,7296]{1,0:T(8,128)(2,1)S(1)}, bf16[16,7296]{1,0:T(8,128)(2,1)S(1)}, u32[]{:S(2)}, u32[]{:S(2)}) collective-permute-start(bf16[16,7296]{1,0:T(8,128)(2,1)S(1)} %slice.53), channel_id=1, source_target_pairs={{0,96},{1,25},{2,98},{3,27},{4,100},{5,29},{6,102},{7,31},{8,104},... | collective-permute-start | bytes 700424 | tf_op jit(solution)/shard_map/ppermute | solution.py:37
  63.3 2.9 %collective-permute-done.18.refs_3_.refs_11_ = bf16[16,7296]{1,0:T(8,128)(2,1)S(1)} collective-permute-done((bf16[16,7296]{1,0:T(8,128)(2,1)S(1)}, bf16[16,7296]{1,0:T(8,128)(2,1)S(1)}, u32[]{:S(2)}, u32[]{:S(2)}) %collective-permute-start.18) | collective-permute-done | bytes 233504 | tf_op jit(solution)/shard_map/ppermute | solution.py:37
  66.3 3.5 %collective-permute-start.17 = (bf16[48,7296]{1,0:T(8,128)(2,1)}, bf16[48,7296]{1,0:T(8,128)(2,1)}, u32[]{:S(2)}, u32[]{:S(2)}) collective-permute-start(bf16[48,7296]{1,0:T(8,128)(2,1)} %slice.52), channel_id=1, source_target_pairs={{0,96},{1,25},{2,98},{3,27},{4,100},{5,29},{6,102},{7,31},{8,104},... | collective-permute-start | bytes 2101256 | tf_op jit(solution)/shard_map/ppermute | solution.py:37
  69.7 1.9 %collective-permute-done.15.refs_0_.refs_8_ = bf16[48,7296]{1,0:T(8,128)(2,1)} collective-permute-done((bf16[48,7296]{1,0:T(8,128)(2,1)}, bf16[48,7296]{1,0:T(8,128)(2,1)}, u32[]{:S(2)}, u32[]{:S(2)}) %collective-permute-start.15) | collective-permute-done | bytes 700448 | tf_op jit(solution)/shard_map/ppermute | solution.py:37
  73.7 9.3 %first_hidden.1 = (bf16[256,512]{1,0:T(8,128)(2,1)S(1)}, bf16[2,7168,256]{2,1,0:T(8,128)(2,1)S(1)}, bf16[2,7168,256]{2,1,0:T(8,128)(2,1)S(1)}, bf16[2,256,7168]{2,1,0:T(8,128)(2,1)S(1)}) custom-call(s32[1]{0:T(128)} %bitcast.first_ref, bf16[96,7296]{1,0:T(8,128)(2,1)} %pack.4.refs_0_, bf16[32,7296]{1,0:T(8,128)(2,1)S(1)} %copy-done.2, ...), custom_call_target="tpu_custom_call" | custom-call | flops 3758096384 | bytes 22020096 | tf_op jit(solution)/shard_map/first_hidden/pallas_call | solution.py:196
  83.9 5.3 %hidden.3.refs_0_ = bf16[256,512]{1,0:T(8,128)(2,1)S(1)} custom-call(s32[1]{0:T(128)} %bitcast.first_ref, bf16[96,7296]{1,0:T(8,128)(2,1)} %collective-permute-done.10.refs_0_.refs_4_, bf16[32,7296]{1,0:T(8,128)(2,1)S(1)} %collective-permute-done.12.refs_1_.refs_5_, bf16[96,7296]{1,0:T(8,128)(2,1)S(1)} %collective-permute-done.13.refs_2_.refs_6_, ...), custom_call_target="tpu_custom_call" | custom-call | flops 3758096384 | bytes 18350080 | tf_op jit(solution)/shard_map/hidden/pallas_call | solution.py:252
  89.9 5.7 %hidden.4.refs_0_ = bf16[256,512]{1,0:T(8,128)(2,1)S(1)} custom-call(s32[1]{0:T(128)} %bitcast.first_ref, bf16[96,7296]{1,0:T(8,128)(2,1)} %collective-permute-done.11.refs_0_.refs_4_, bf16[32,7296]{1,0:T(8,128)(2,1)S(1)} %collective-permute-done.23.refs_1_.refs_5_, bf16[96,7296]{1,0:T(8,128)(2,1)} %collective-permute-done.24.refs_2_.refs_6_, ...), custom_call_target="tpu_custom_call" | custom-call | flops 3758096384 | bytes 18350080 | tf_op jit(solution)/shard_map/hidden/pallas_call | solution.py:252
  95.6 5.3 %hidden.5.refs_0_ = bf16[256,512]{1,0:T(8,128)(2,1)S(1)} custom-call(s32[1]{0:T(128)} %bitcast.first_ref, bf16[48,7296]{1,0:T(8,128)(2,1)} %collective-permute-done.15.refs_0_.refs_8_, bf16[16,7296]{1,0:T(8,128)(2,1)S(1)} %copy-done.4, bf16[48,7296]{1,0:T(8,128)(2,1)} %collective-permute-done.17.refs_2_.refs_10_, bf16[16,7296]{1,0:T(8,128)(2,1)S(1)} %copy-done.6, ...), custom_call_target="tpu_custom_call" | custom-call | flops 3758096384 | bytes 18350080 | tf_op jit(solution)/shard_map/hidden/pallas_call | solution.py:252
  102.4 2.5 %outputs.9 = bf16[256,7168]{1,0:T(8,128)(2,1)S(1)} custom-call(bf16[256,512]{1,0:T(8,128)(2,1)S(1)} %hidden.4.refs_0_, bf16[2,256,7168]{2,1,0:T(8,128)(2,1)S(1)} %get-tuple-element.31.refs_1_), custom_call_target="tpu_custom_call" | custom-call | flops 1879048192 | bytes 14680064 | tf_op jit(solution)/shard_map/outputs/pallas_call | solution.py:307
  107.3 6.7 %collective-permute-done.27.refs_2_ = bf16[128,7168]{1,0:T(8,128)(2,1)S(1)} collective-permute-done((bf16[128,7168]{1,0:T(8,128)(2,1)S(1)}, bf16[128,7168]{1,0:T(8,128)(2,1)S(1)}, u32[]{:S(2)}, u32[]{:S(2)}) %collective-permute-start.27) | collective-permute-done | bytes 1835040 | tf_op jit(solution)/shard_map/ppermute | solution.py:41
  117.7 2.8 %outputs.10 = (bf16[48,7168]{1,0:T(8,128)(2,1)S(1)}, bf16[48,7168]{1,0:T(8,128)(2,1)S(1)}, bf16[32,7168]{1,0:T(8,128)(2,1)S(1)}, bf16[48,7168]{1,0:T(8,128)(2,1)...) custom-call(bf16[256,512]{1,0:T(8,128)(2,1)S(1)} %hidden.3.refs_0_, ...), custom_call_target="tpu_custom_call" | custom-call | flops 1879048192 | bytes 14680064 | tf_op jit(solution)/shard_map/outputs/pallas_call | solution.py:307
  120.6 8.5 %collective-permute-done.28.via_ref = bf16[64,7168]{1,0:T(8,128)(2,1)S(1)} collective-permute-done((bf16[64,7168]{1,0:T(8,128)(2,1)S(1)}, bf16[64,7168]{1,0:T(8,128)(2,1)S(1)}, u32[]{:S(2)}, u32[]{:S(2)}) %collective-permute-start.28) | collective-permute-done | bytes 917536 | tf_op jit(solution)/shard_map/ppermute | solution.py:37
  129.2 2.8 %collective-permute-start.34 = (bf16[32,7168]{1,0:T(8,128)(2,1)S(1)}, bf16[32,7168]{1,0:T(8,128)(2,1)S(1)}, u32[]{:S(2)}, u32[]{:S(2)}) collective-permute-start(bf16[32,7168]{1,0:T(8,128)(2,1)S(1)} %merge.6), channel_id=1, source_target_pairs={{0,96},{1,25},{2,98},{3,27},{4,100},{5,29},{6,102},{7,31},{8,104},... | collective-permute-start | bytes 1376264 | tf_op jit(solution)/shard_map/ppermute | solution.py:37
  134.2 3.3 %collective-permute-start.29 = (bf16[48,7168]{1,0:T(8,128)(2,1)S(1)}, bf16[48,7168]{1,0:T(8,128)(2,1)S(1)}, u32[]{:S(2)}, u32[]{:S(2)}) collective-permute-start(bf16[48,7168]{1,0:T(8,128)(2,1)S(1)} %merge.4), channel_id=1, source_target_pairs={{0,96},{1,25},{2,98},{3,27},{4,100},{5,29},{6,102},{7,31},{8,104},... | collective-permute-start | bytes 2064392 | tf_op jit(solution)/shard_map/ppermute | solution.py:37
  138.0 3.7 %collective-permute-start.31 = (bf16[48,7168]{1,0:T(8,128)(2,1)S(1)}, bf16[48,7168]{1,0:T(8,128)(2,1)S(1)}, u32[]{:S(2)}, u32[]{:S(2)}) collective-permute-start(bf16[48,7168]{1,0:T(8,128)(2,1)S(1)} %get-tuple-element.49), channel_id=1, source_target_pairs={{0,96},{1,25},{2,98},{3,27},{4,100},{5,29},{6,102},{7,31},{8,104},... | collective-permute-start | bytes 2064392 | tf_op jit(solution)/shard_map/ppermute | solution.py:37
  142.0 2.9 %collective-permute-start.36 = (bf16[16,7168]{1,0:T(8,128)(2,1)S(1)}, bf16[16,7168]{1,0:T(8,128)(2,1)S(1)}, u32[]{:S(2)}, u32[]{:S(2)}) collective-permute-start(bf16[16,7168]{1,0:T(8,128)(2,1)S(1)} %get-tuple-element.62), channel_id=1, source_target_pairs={{0,24},{1,7},{2,26},{3,1},{4,28},{5,3},{6,30},{7,5},{8,0},{9,15},{... | collective-permute-start | bytes 688136 | tf_op jit(solution)/shard_map/ppermute | solution.py:37
  145.0 6.0 %collective-permute-done.36.refs_6_ = bf16[16,7168]{1,0:T(8,128)(2,1)S(1)} collective-permute-done((bf16[16,7168]{1,0:T(8,128)(2,1)S(1)}, bf16[16,7168]{1,0:T(8,128)(2,1)S(1)}, u32[]{:S(2)}, u32[]{:S(2)}) %collective-permute-start.36) | collective-permute-done | bytes 229408 | tf_op jit(solution)/shard_map/ppermute | solution.py:37
  152.6 6.1 %collective-permute-done.37.refs_7_ = bf16[16,7168]{1,0:T(8,128)(2,1)S(1)} collective-permute-done((bf16[16,7168]{1,0:T(8,128)(2,1)S(1)}, bf16[16,7168]{1,0:T(8,128)(2,1)S(1)}, u32[]{:S(2)}, u32[]{:S(2)}) %collective-permute-start.37) | collective-permute-done | bytes 229408 | tf_op jit(solution)/shard_map/ppermute | solution.py:37
  159.3 2.1 %collective-permute-start.38 = (bf16[32,7168]{1,0:T(8,128)(2,1)S(1)}, bf16[32,7168]{1,0:T(8,128)(2,1)S(1)}, u32[]{:S(2)}, u32[]{:S(2)}) collective-permute-start(bf16[32,7168]{1,0:T(8,128)(2,1)S(1)} %get-tuple-element.56), channel_id=1, source_target_pairs={{0,24},{1,7},{2,26},{3,1},{4,28},{5,3},{6,30},{7,5},{8,0},{9,15},{... | collective-permute-start | bytes 1376264 | tf_op jit(solution)/shard_map/ppermute | solution.py:37
  162.0 5.8 %collective-permute-done.38 = bf16[32,7168]{1,0:T(8,128)(2,1)S(1)} collective-permute-done((bf16[32,7168]{1,0:T(8,128)(2,1)S(1)}, bf16[32,7168]{1,0:T(8,128)(2,1)S(1)}, u32[]{:S(2)}, u32[]{:S(2)}) %collective-permute-start.38) | collective-permute-done | bytes 458784 | tf_op jit(solution)/shard_map/ppermute | solution.py:37
  167.8 3.2 %collective-permute-done.39 = bf16[32,7168]{1,0:T(8,128)(2,1)S(1)} collective-permute-done((bf16[32,7168]{1,0:T(8,128)(2,1)S(1)}, bf16[32,7168]{1,0:T(8,128)(2,1)S(1)}, u32[]{:S(2)}, u32[]{:S(2)}) %collective-permute-start.39) | collective-permute-done | bytes 458784 | tf_op jit(solution)/shard_map/ppermute | solution.py:37
  171.3 2.1 %collective-permute-start.40 = (bf16[8,7168]{1,0:T(8,128)(2,1)S(1)}, bf16[8,7168]{1,0:T(8,128)(2,1)S(1)}, u32[]{:S(2)}, u32[]{:S(2)}) collective-permute-start(bf16[8,7168]{1,0:T(8,128)(2,1)S(1)} %get-tuple-element.58), channel_id=1, source_target_pairs={{0,6},{1,97},{2,0},{3,99},{4,2},{5,101},{6,4},{7,103},{8,14},{9,10... | collective-permute-start | bytes 344072 | tf_op jit(solution)/shard_map/ppermute | solution.py:37
  173.4 1.9 %collective-permute-start.42 = (bf16[8,7168]{1,0:T(8,128)(2,1)S(1)}, bf16[8,7168]{1,0:T(8,128)(2,1)S(1)}, u32[]{:S(2)}, u32[]{:S(2)}) collective-permute-start(bf16[8,7168]{1,0:T(8,128)(2,1)S(1)} %get-tuple-element.59), channel_id=1, source_target_pairs={{0,4},{1,65},{2,6},{3,67},{4,0},{5,69},{6,2},{7,71},{8,12},{9,73},... | collective-permute-start | bytes 344072 | tf_op jit(solution)/shard_map/ppermute | solution.py:37
  176.9 3.7 %collective-permute-done.41 = bf16[8,7168]{1,0:T(8,128)(2,1)S(1)} collective-permute-done((bf16[8,7168]{1,0:T(8,128)(2,1)S(1)}, bf16[8,7168]{1,0:T(8,128)(2,1)S(1)}, u32[]{:S(2)}, u32[]{:S(2)}) %collective-permute-start.41) | collective-permute-done | bytes 114720 | tf_op jit(solution)/shard_map/ppermute | solution.py:37
  (119 shorter events, 43.0 us)
Async XLA Ops:
  14.1 9.8 %collective-permute-start.3 = (bf16[32,7296]{1,0:T(8,128)(2,1)S(1)}, bf16[32,7296]{1,0:T(8,128)(2,1)S(1)}, u32[]{:S(2)}, u32[]{:S(2)}) collective-permute-start(bf16[32,7296]{1,0:T(8,128)(2,1)S(1)} %pack.3.refs_0_), channel_id=1, source_target_pairs={{0,8},{1,3},{2,10},{3,5},{4,12},{5,7},{6,14},{7,1},{8,16},{9,11},{... | collective-permute-start | bytes 1400840 | tf_op jit(solution)/shard_map/ppermute | solution.py:37
  15.7 8.6 %collective-permute-start.4 = (bf16[32,7296]{1,0:T(8,128)(2,1)S(1)}, bf16[32,7296]{1,0:T(8,128)(2,1)S(1)}, u32[]{:S(2)}, u32[]{:S(2)}) collective-permute-start(bf16[32,7296]{1,0:T(8,128)(2,1)S(1)} %pack.3.refs_0_), channel_id=1, source_target_pairs={{0,24},{1,7},{2,26},{3,1},{4,28},{5,3},{6,30},{7,5},{8,0},{9,15},{... | collective-permute-start | bytes 1400840 | tf_op jit(solution)/shard_map/ppermute | solution.py:37
  25.5 26.5 %collective-permute-start.10 = (bf16[96,7296]{1,0:T(8,128)(2,1)}, bf16[96,7296]{1,0:T(8,128)(2,1)}, u32[]{:S(2)}, u32[]{:S(2)}) collective-permute-start(bf16[96,7296]{1,0:T(8,128)(2,1)} %pack.4.refs_0_), channel_id=1, source_target_pairs={{0,32},{1,9},{2,34},{3,11},{4,36},{5,13},{6,38},{7,15},{8,40},{9,1... | collective-permute-start | bytes 4202504 | tf_op jit(solution)/shard_map/ppermute | solution.py:37
  27.0 32.4 %collective-permute-start.13 = (bf16[96,7296]{1,0:T(8,128)(2,1)}, bf16[96,7296]{1,0:T(8,128)(2,1)S(1)}, u32[]{:S(2)}, u32[]{:S(2)}) collective-permute-start(bf16[96,7296]{1,0:T(8,128)(2,1)} %pack.4.refs_0_), channel_id=1, source_target_pairs={{0,96},{1,25},{2,98},{3,27},{4,100},{5,29},{6,102},{7,31},{8,104},... | collective-permute-start | bytes 4202504 | tf_op jit(solution)/shard_map/ppermute | solution.py:37
  28.8 9.8 %collective-permute-start.5 = (bf16[16,7296]{1,0:T(8,128)(2,1)S(1)}, bf16[16,7296]{1,0:T(8,128)(2,1)S(1)}, u32[]{:S(2)}, u32[]{:S(2)}) collective-permute-start(bf16[16,7296]{1,0:T(8,128)(2,1)S(1)} %slice.48), channel_id=1, source_target_pairs={{0,8},{1,3},{2,10},{3,5},{4,12},{5,7},{6,14},{7,1},{8,16},{9,11},{... | collective-permute-start | bytes 700424 | tf_op jit(solution)/shard_map/ppermute | solution.py:37
  30.4 8.6 %collective-permute-start.6 = (bf16[16,7296]{1,0:T(8,128)(2,1)S(1)}, bf16[16,7296]{1,0:T(8,128)(2,1)S(1)}, u32[]{:S(2)}, u32[]{:S(2)}) collective-permute-start(bf16[16,7296]{1,0:T(8,128)(2,1)S(1)} %slice.49), channel_id=1, source_target_pairs={{0,24},{1,7},{2,26},{3,1},{4,28},{5,3},{6,30},{7,5},{8,0},{9,15},{... | collective-permute-start | bytes 700424 | tf_op jit(solution)/shard_map/ppermute | solution.py:37
  39.1 11.4 %collective-permute-start.12 = (bf16[32,7296]{1,0:T(8,128)(2,1)S(1)}, bf16[32,7296]{1,0:T(8,128)(2,1)S(1)}, u32[]{:S(2)}, u32[]{:S(2)}) collective-permute-start(bf16[32,7296]{1,0:T(8,128)(2,1)S(1)} %pack.5.refs_1_), channel_id=1, source_target_pairs={{0,32},{1,9},{2,34},{3,11},{4,36},{5,13},{6,38},{7,15},{8,40},{9,1... | collective-permute-start | bytes 1400840 | tf_op jit(solution)/shard_map/ppermute | solution.py:37
  39.5 30.3 %collective-permute-start.7 = (bf16[96,7296]{1,0:T(8,128)(2,1)}, bf16[96,7296]{1,0:T(8,128)(2,1)}, u32[]{:S(2)}, u32[]{:S(2)}) collective-permute-start(bf16[96,7296]{1,0:T(8,128)(2,1)} %pack.4.refs_0_), channel_id=1, source_target_pairs={{0,1},{1,0},{2,3},{3,2},{4,5},{5,4},{6,7},{7,6},{8,9},{9,8},{10,11... | collective-permute-start | bytes 4202504 | tf_op jit(solution)/shard_map/ppermute | solution.py:41
  39.5 12.6 %collective-permute-start.8 = (bf16[32,7296]{1,0:T(8,128)(2,1)S(1)}, bf16[32,7296]{1,0:T(8,128)(2,1)S(1)}, u32[]{:S(2)}, u32[]{:S(2)}) collective-permute-start(bf16[32,7296]{1,0:T(8,128)(2,1)S(1)} %pack.5.refs_1_), channel_id=1, source_target_pairs={{0,1},{1,0},{2,3},{3,2},{4,5},{5,4},{6,7},{7,6},{8,9},{9,8},{10,11... | collective-permute-start | bytes 1400840 | tf_op jit(solution)/shard_map/ppermute | solution.py:41
  50.5 8.6 %collective-permute-start.14 = (bf16[32,7296]{1,0:T(8,128)(2,1)S(1)}, bf16[32,7296]{1,0:T(8,128)(2,1)S(1)}, u32[]{:S(2)}, u32[]{:S(2)}) collective-permute-start(bf16[32,7296]{1,0:T(8,128)(2,1)S(1)} %pack.5.refs_1_), channel_id=1, source_target_pairs={{0,96},{1,25},{2,98},{3,27},{4,100},{5,29},{6,102},{7,31},{8,104},... | collective-permute-start | bytes 1400840 | tf_op jit(solution)/shard_map/ppermute | solution.py:37
  52.1 31.5 %collective-permute-start.11 = (bf16[96,7296]{1,0:T(8,128)(2,1)}, bf16[96,7296]{1,0:T(8,128)(2,1)}, u32[]{:S(2)}, u32[]{:S(2)}) collective-permute-start(bf16[96,7296]{1,0:T(8,128)(2,1)} %collective-permute-done.10.refs_0_.refs_4_), channel_id=1, source_target_pairs={{0,1},{1,0},{2,3},{3,2},{4,5},{5,4},{6,7},{7,6},{8,9},{9,8},{10,11... | collective-permute-start | bytes 4202504 | tf_op jit(solution)/shard_map/ppermute | solution.py:41
  59.1 12.6 %collective-permute-start.15 = (bf16[48,7296]{1,0:T(8,128)(2,1)}, bf16[48,7296]{1,0:T(8,128)(2,1)}, u32[]{:S(2)}, u32[]{:S(2)}) collective-permute-start(bf16[48,7296]{1,0:T(8,128)(2,1)} %slice.50), channel_id=1, source_target_pairs={{0,32},{1,9},{2,34},{3,11},{4,36},{5,13},{6,38},{7,15},{8,40},{9,1... | collective-permute-start | bytes 2101256 | tf_op jit(solution)/shard_map/ppermute | solution.py:37
  59.4 30.5 %collective-permute-start.24 = (bf16[96,7296]{1,0:T(8,128)(2,1)S(1)}, bf16[96,7296]{1,0:T(8,128)(2,1)}, u32[]{:S(2)}, u32[]{:S(2)}) collective-permute-start(bf16[96,7296]{1,0:T(8,128)(2,1)S(1)} %collective-permute-done.13.refs_2_.refs_6_), channel_id=1, source_target_pairs={{0,1},{1,0},{2,3},{3,2},{4,5},{5,4},{6,7},{7,6},{8,9},{9,8},{10,11... | collective-permute-start | bytes 4202504 | tf_op jit(solution)/shard_map/ppermute | solution.py:41
  66.3 16.7 %collective-permute-start.17 = (bf16[48,7296]{1,0:T(8,128)(2,1)}, bf16[48,7296]{1,0:T(8,128)(2,1)}, u32[]{:S(2)}, u32[]{:S(2)}) collective-permute-start(bf16[48,7296]{1,0:T(8,128)(2,1)} %slice.52), channel_id=1, source_target_pairs={{0,96},{1,25},{2,98},{3,27},{4,100},{5,29},{6,102},{7,31},{8,104},... | collective-permute-start | bytes 2101256 | tf_op jit(solution)/shard_map/ppermute | solution.py:37
  69.7 19.5 %collective-permute-start.23 = (bf16[32,7296]{1,0:T(8,128)(2,1)S(1)}, bf16[32,7296]{1,0:T(8,128)(2,1)S(1)}, u32[]{:S(2)}, u32[]{:S(2)}) collective-permute-start(bf16[32,7296]{1,0:T(8,128)(2,1)S(1)} %collective-permute-done.12.refs_1_.refs_5_), channel_id=1, source_target_pairs={{0,1},{1,0},{2,3},{3,2},{4,5},{5,4},{6,7},{7,6},{8,9},{9,8},{10,11... | collective-permute-start | bytes 1400840 | tf_op jit(solution)/shard_map/ppermute | solution.py:41
  71.7 17.9 %collective-permute-start.25 = (bf16[32,7296]{1,0:T(8,128)(2,1)S(1)}, bf16[32,7296]{1,0:T(8,128)(2,1)S(1)}, u32[]{:S(2)}, u32[]{:S(2)}) collective-permute-start(bf16[32,7296]{1,0:T(8,128)(2,1)S(1)} %collective-permute-done.14.refs_3_.refs_7_), channel_id=1, source_target_pairs={{0,1},{1,0},{2,3},{3,2},{4,5},{5,4},{6,7},{7,6},{8,9},{9,8},{10,11... | collective-permute-start | bytes 1400840 | tf_op jit(solution)/shard_map/ppermute | solution.py:41
  83.0 12.6 %collective-permute-start.19 = (bf16[48,7296]{1,0:T(8,128)(2,1)}, bf16[48,7296]{1,0:T(8,128)(2,1)S(1)}, u32[]{:S(2)}, u32[]{:S(2)}) collective-permute-start(bf16[48,7296]{1,0:T(8,128)(2,1)} %collective-permute-done.15.refs_0_.refs_8_), channel_id=1, source_target_pairs={{0,1},{1,0},{2,3},{3,2},{4,5},{5,4},{6,7},{7,6},{8,9},{9,8},{10,11... | collective-permute-start | bytes 2101256 | tf_op jit(solution)/shard_map/ppermute | solution.py:41
  83.6 12.0 %collective-permute-start.21 = (bf16[48,7296]{1,0:T(8,128)(2,1)}, bf16[48,7296]{1,0:T(8,128)(2,1)S(1)}, u32[]{:S(2)}, u32[]{:S(2)}) collective-permute-start(bf16[48,7296]{1,0:T(8,128)(2,1)} %collective-permute-done.17.refs_2_.refs_10_), channel_id=1, source_target_pairs={{0,1},{1,0},{2,3},{3,2},{4,5},{5,4},{6,7},{7,6},{8,9},{9,8},{10,11... | collective-permute-start | bytes 2101256 | tf_op jit(solution)/shard_map/ppermute | solution.py:41
  104.9 12.8 %collective-permute-start.26 = (bf16[256,7168]{1,0:T(8,128)(2,1)S(1)}, bf16[256,7168]{1,0:T(8,128)(2,1)S(1)}, u32[]{:S(2)}, u32[]{:S(2)}) collective-permute-start(bf16[256,7168]{1,0:T(8,128)(2,1)S(1)} %outputs.9), channel_id=1, source_target_pairs={{0,1},{1,0},{2,3},{3,2},{4,5},{5,4},{6,7},{7,6},{8,9},{9,8},{10,11... | collective-permute-start | bytes 11010056 | tf_op jit(solution)/shard_map/ppermute | solution.py:41
  105.2 8.8 %collective-permute-start.27 = (bf16[128,7168]{1,0:T(8,128)(2,1)S(1)}, bf16[128,7168]{1,0:T(8,128)(2,1)S(1)}, u32[]{:S(2)}, u32[]{:S(2)}) collective-permute-start(bf16[128,7168]{1,0:T(8,128)(2,1)S(1)} %outputs.8), channel_id=1, source_target_pairs={{0,1},{1,0},{2,3},{3,2},{4,5},{5,4},{6,7},{7,6},{8,9},{9,8},{10,11... | collective-permute-start | bytes 5505032 | tf_op jit(solution)/shard_map/ppermute | solution.py:41
  107.0 25.2 %collective-permute-start.9 = (bf16[128,7168]{1,0:T(8,128)(2,1)S(1)}, bf16[128,7168]{1,0:T(8,128)(2,1)S(1)}, u32[]{:S(2)}, u32[]{:S(2)}) collective-permute-start(bf16[128,7168]{1,0:T(8,128)(2,1)S(1)} %outputs.6), channel_id=1, source_target_pairs={{0,1},{1,0},{2,3},{3,2},{4,5},{5,4},{6,7},{7,6},{8,9},{9,8},{10,11... | collective-permute-start | bytes 5505032 | tf_op jit(solution)/shard_map/ppermute | solution.py:41
  115.6 13.5 %collective-permute-start.28 = (bf16[64,7168]{1,0:T(8,128)(2,1)S(1)}, bf16[64,7168]{1,0:T(8,128)(2,1)S(1)}, u32[]{:S(2)}, u32[]{:S(2)}) collective-permute-start(bf16[64,7168]{1,0:T(8,128)(2,1)S(1)} %get-tuple-element.46), channel_id=1, source_target_pairs={{0,96},{1,25},{2,98},{3,27},{4,100},{5,29},{6,102},{7,31},{8,104},... | collective-permute-start | bytes 2752520 | tf_op jit(solution)/shard_map/ppermute | solution.py:37
  117.3 14.7 %collective-permute-start.32 = (bf16[64,7168]{1,0:T(8,128)(2,1)S(1)}, bf16[64,7168]{1,0:T(8,128)(2,1)S(1)}, u32[]{:S(2)}, u32[]{:S(2)}) collective-permute-start(bf16[64,7168]{1,0:T(8,128)(2,1)S(1)} %get-tuple-element.51), channel_id=1, source_target_pairs={{0,32},{1,9},{2,34},{3,11},{4,36},{5,13},{6,38},{7,15},{8,40},{9,1... | collective-permute-start | bytes 2752520 | tf_op jit(solution)/shard_map/ppermute | solution.py:37
  129.2 8.8 %collective-permute-start.34 = (bf16[32,7168]{1,0:T(8,128)(2,1)S(1)}, bf16[32,7168]{1,0:T(8,128)(2,1)S(1)}, u32[]{:S(2)}, u32[]{:S(2)}) collective-permute-start(bf16[32,7168]{1,0:T(8,128)(2,1)S(1)} %merge.6), channel_id=1, source_target_pairs={{0,96},{1,25},{2,98},{3,27},{4,100},{5,29},{6,102},{7,31},{8,104},... | collective-permute-start | bytes 1376264 | tf_op jit(solution)/shard_map/ppermute | solution.py:37
  132.1 9.8 %collective-permute-start.35 = (bf16[32,7168]{1,0:T(8,128)(2,1)S(1)}, bf16[32,7168]{1,0:T(8,128)(2,1)S(1)}, u32[]{:S(2)}, u32[]{:S(2)}) collective-permute-start(bf16[32,7168]{1,0:T(8,128)(2,1)S(1)} %merge.7), channel_id=1, source_target_pairs={{0,32},{1,9},{2,34},{3,11},{4,36},{5,13},{6,38},{7,15},{8,40},{9,1... | collective-permute-start | bytes 1376264 | tf_op jit(solution)/shard_map/ppermute | solution.py:37
  134.0 24.7 %collective-permute-start.33 = (bf16[48,7168]{1,0:T(8,128)(2,1)S(1)}, bf16[48,7168]{1,0:T(8,128)(2,1)S(1)}, u32[]{:S(2)}, u32[]{:S(2)}) collective-permute-start(bf16[48,7168]{1,0:T(8,128)(2,1)S(1)} %merge.5), channel_id=1, source_target_pairs={{0,32},{1,9},{2,34},{3,11},{4,36},{5,13},{6,38},{7,15},{8,40},{9,1... | collective-permute-start | bytes 2064392 | tf_op jit(solution)/shard_map/ppermute | solution.py:37
  134.2 24.4 %collective-permute-start.29 = (bf16[48,7168]{1,0:T(8,128)(2,1)S(1)}, bf16[48,7168]{1,0:T(8,128)(2,1)S(1)}, u32[]{:S(2)}, u32[]{:S(2)}) collective-permute-start(bf16[48,7168]{1,0:T(8,128)(2,1)S(1)} %merge.4), channel_id=1, source_target_pairs={{0,96},{1,25},{2,98},{3,27},{4,100},{5,29},{6,102},{7,31},{8,104},... | collective-permute-start | bytes 2064392 | tf_op jit(solution)/shard_map/ppermute | solution.py:37
  137.5 21.2 %collective-permute-start.30 = (bf16[48,7168]{1,0:T(8,128)(2,1)S(1)}, bf16[48,7168]{1,0:T(8,128)(2,1)S(1)}, u32[]{:S(2)}, u32[]{:S(2)}) collective-permute-start(bf16[48,7168]{1,0:T(8,128)(2,1)S(1)} %get-tuple-element.47), channel_id=1, source_target_pairs={{0,32},{1,9},{2,34},{3,11},{4,36},{5,13},{6,38},{7,15},{8,40},{9,1... | collective-permute-start | bytes 2064392 | tf_op jit(solution)/shard_map/ppermute | solution.py:37
  138.0 20.7 %collective-permute-start.31 = (bf16[48,7168]{1,0:T(8,128)(2,1)S(1)}, bf16[48,7168]{1,0:T(8,128)(2,1)S(1)}, u32[]{:S(2)}, u32[]{:S(2)}) collective-permute-start(bf16[48,7168]{1,0:T(8,128)(2,1)S(1)} %get-tuple-element.49), channel_id=1, source_target_pairs={{0,96},{1,25},{2,98},{3,27},{4,100},{5,29},{6,102},{7,31},{8,104},... | collective-permute-start | bytes 2064392 | tf_op jit(solution)/shard_map/ppermute | solution.py:37
  142.0 8.9 %collective-permute-start.36 = (bf16[16,7168]{1,0:T(8,128)(2,1)S(1)}, bf16[16,7168]{1,0:T(8,128)(2,1)S(1)}, u32[]{:S(2)}, u32[]{:S(2)}) collective-permute-start(bf16[16,7168]{1,0:T(8,128)(2,1)S(1)} %get-tuple-element.62), channel_id=1, source_target_pairs={{0,24},{1,7},{2,26},{3,1},{4,28},{5,3},{6,30},{7,5},{8,0},{9,15},{... | collective-permute-start | bytes 688136 | tf_op jit(solution)/shard_map/ppermute | solution.py:37
  159.3 8.5 %collective-permute-start.38 = (bf16[32,7168]{1,0:T(8,128)(2,1)S(1)}, bf16[32,7168]{1,0:T(8,128)(2,1)S(1)}, u32[]{:S(2)}, u32[]{:S(2)}) collective-permute-start(bf16[32,7168]{1,0:T(8,128)(2,1)S(1)} %get-tuple-element.56), channel_id=1, source_target_pairs={{0,24},{1,7},{2,26},{3,1},{4,28},{5,3},{6,30},{7,5},{8,0},{9,15},{... | collective-permute-start | bytes 1376264 | tf_op jit(solution)/shard_map/ppermute | solution.py:37
  161.4 9.7 %collective-permute-start.39 = (bf16[32,7168]{1,0:T(8,128)(2,1)S(1)}, bf16[32,7168]{1,0:T(8,128)(2,1)S(1)}, u32[]{:S(2)}, u32[]{:S(2)}) collective-permute-start(bf16[32,7168]{1,0:T(8,128)(2,1)S(1)} %get-tuple-element.57), channel_id=1, source_target_pairs={{0,8},{1,3},{2,10},{3,5},{4,12},{5,7},{6,14},{7,1},{8,16},{9,11},{... | collective-permute-start | bytes 1376264 | tf_op jit(solution)/shard_map/ppermute | solution.py:37
  (26 other events, 308.0 us)
